TPU v7x, 512 devices: a whole 4x4x16 slice. The times are simulated.
512 devices in a mesh: seq: 64 (over z, y), tp: 8 (over x, core).
Axes of the slice: x: 4, y: 4, z: 16, core: 2. Of those that a mesh axis runs over, the one named last changes fastest.
Arguments:
- features: float32 [3, 4096, 16384], P(None, 'tp', 'seq'), may hold values from -6 to 6
- short_filter: float32 [3, 256, 7], P(None, 'tp'), may hold values from -2 to 2
- medium_filter: float32 [3, 256, 128], P(None, 'tp'), may hold values from -0.5 to 0.5
- rates: float32 [256, 16], P('tp'), as said below
- residues: float32 [256, 16], P('tp'), may hold values from -1.5 to 1.5
- skip_gain: float32 [4096], P('tp'), may hold values from -4 to 4
- out_weight: bfloat16 [2048, 4096], P(None, 'tp'), may hold values from -0.125 to 0.125
Outputs:
- mixed: float32 [2048, 16384], P('tp', 'seq')
Inputs may be any that keep to these rules, and one draw needn't show every extreme that they name: `rates`: every rate lies between 1 / 163840 and 1 / 20.
All inputs are finite; a program needn't handle non-finite values.
Results may differ from a plain program's by a relative error of at most 0.0029.
Values sent between devices are 32-bit elements; how exact they have to be, the bound alone decides.
A program may use at most 128 MiB of HBM per device.

v0:
```python
import jax
import jax.numpy as jnp
from jax import lax
from jax.sharding import PartitionSpec as P

GROUP = 16
SHORT = 7
MEDIUM = 128


def passed_along(block, axis, distance):
    devices = range(lax.axis_size(axis))
    route = [(i - distance, i) for i in devices if i - distance in devices]
    return lax.ppermute(block, axis, route)


def prefix_2(value, axis, join, neutral):
    count, mine = (lax.axis_size(axis), lax.axis_index(axis))
    pieces = jax.tree.map(lambda part: lax.all_gather(part, axis), value)
    so_far = jax.tree.map(
        lambda part, zero: jnp.full_like(part, 0) + jnp.asarray(zero, part.dtype), value, neutral
    )

    def lap(position, so_far):
        longer = join(so_far, jax.tree.map(lambda part: part[position], pieces))
        return jax.tree.map(lambda new, old: jnp.where(position < mine, new, old), longer, so_far)

    return lax.fori_loop(0, count - 1, lap, so_far)


def short_conv(extended, filters, length):
    coeffs = jnp.repeat(filters, GROUP, axis=1)
    summed = jnp.zeros(extended.shape[:-1] + (length,), extended.dtype)
    for offset in range(SHORT):
        first = SHORT - 1 - offset
        summed = summed + coeffs[:, :, offset : offset + 1] * extended[:, :, first : first + length]
    return summed


def medium_matrix(coeffs):
    block_len = coeffs.shape[0]
    pattern = jnp.concatenate([coeffs[::-1], jnp.zeros((block_len,), coeffs.dtype)])
    return jnp.tile(pattern, block_len)[: block_len * (2 * block_len - 1)].reshape(
        block_len, 2 * block_len - 1
    )


def medium_branch(operands):
    extended, coeffs = operands
    block_len = coeffs.shape[1]
    channels = extended.shape[0]
    groups = coeffs.shape[0]
    length = extended.shape[1] - (block_len - 1)
    block_count = length // block_len
    padded = jnp.concatenate([jnp.zeros((channels, 1), extended.dtype), extended], axis=1)
    blocks = padded.reshape(channels, block_count + 1, block_len)
    windows = jnp.concatenate([blocks[:, :-1], blocks[:, 1:]], axis=2)[:, :, 1:]
    windows = windows.reshape(groups, channels // groups, block_count, 2 * block_len - 1)
    matrices = jax.vmap(medium_matrix)(coeffs)
    result = jnp.einsum("gcbs,gts->gcbt", windows, matrices, precision=lax.Precision.HIGHEST)
    return result.reshape(channels, length)


def long_matrix(kernel):
    block_len = kernel.shape[0]
    pattern = jnp.concatenate(
        [kernel[0:1], jnp.zeros((block_len,), kernel.dtype), kernel[1:][::-1]]
    )
    full = jnp.tile(pattern, block_len)[: block_len * (2 * block_len - 1)].reshape(
        block_len, 2 * block_len - 1
    )
    return full[:, :block_len]


def modal_tables(rates, residues, block_len):
    steps_axis = jnp.arange(block_len).astype(rates.dtype)
    weight = residues * jnp.sqrt(-jnp.expm1(-2.0 * rates))
    decays = jnp.exp(-rates[:, :, None] * steps_axis)
    kernel = jnp.einsum("gn,gnt->gt", weight, decays, precision=lax.Precision.HIGHEST)
    readout = weight[:, :, None] * jnp.exp(-rates[:, :, None] * (steps_axis + 1.0))
    ending = decays[:, :, ::-1]
    return (kernel, readout, ending)


def combine_states(before, behind):
    return (before[0] * behind[0], before[1] * behind[0][:, None, :] + behind[1])


def per_device(features, short_filter, medium_filter, rates, residues, skip_gain, out_weight):
    length = features.shape[2]
    border = passed_along(features[:, :, length - (SHORT - 1) :], "seq", 1)
    shorted = short_conv(jnp.concatenate([border, features], axis=2), short_filter, length)
    trailing = passed_along(shorted[:, :, length - (MEDIUM - 1) :], "seq", 1)
    extended = jnp.concatenate([trailing, shorted], axis=2)
    mediated = lax.map(medium_branch, (extended, medium_filter))
    product = mediated[1] * mediated[2]
    block_len = MEDIUM
    groups = rates.shape[0]
    block_count = length // block_len
    kernel, readout, ending = modal_tables(rates, residues, block_len)
    matrices = jax.vmap(long_matrix)(kernel)
    blocks = product.reshape(groups, GROUP, block_count, block_len)
    inside = jnp.einsum("gcbs,gts->gcbt", blocks, matrices, precision=lax.Precision.HIGHEST)
    finals = jnp.einsum("gcbs,gns->gcbn", blocks, ending, precision=lax.Precision.HIGHEST)
    order_float = jnp.arange(block_count).astype(jnp.float32)
    lagged = jnp.exp(-rates[:, :, None] * block_len * (block_count - 1.0 - order_float))
    shard_state = jnp.einsum("gcbn,gnb->gcn", finals, lagged, precision=lax.Precision.HIGHEST)
    shard_decay = jnp.exp(-rates * float(block_len * block_count))
    prefix = prefix_2(
        (shard_decay, shard_state),
        "seq",
        combine_states,
        (jnp.ones_like(shard_decay), jnp.zeros_like(shard_state)),
    )
    incoming = prefix[1]
    block_ids = jnp.arange(block_count, dtype=jnp.int32)
    block_gap = block_ids[:, None] - block_ids[None, :] - 1
    gap_float = jnp.maximum(block_gap, 0).astype(jnp.float32)
    within = jnp.exp(-rates[:, :, None, None] * block_len * gap_float)
    within = jnp.where((block_gap >= 0)[None, None], within, 0.0)
    earlier = jnp.einsum("gnbe,gcen->gcbn", within, finals, precision=lax.Precision.HIGHEST)
    entering = jnp.exp(-rates[:, :, None] * block_len * order_float)
    states = earlier + incoming[:, :, None, :] * jnp.swapaxes(entering, 1, 2)[:, None]
    carried = jnp.einsum("gcbn,gnt->gcbt", states, readout, precision=lax.Precision.HIGHEST)
    longed = (inside + carried).reshape(product.shape) + skip_gain[:, None] * product
    gated_out = (mediated[0] * longed).astype(jnp.bfloat16)
    return lax.psum_scatter(
        jnp.dot(out_weight, gated_out, preferred_element_type=jnp.float32),
        "tp",
        scatter_dimension=0,
        tiled=True,
    )


def solution(mesh):
    in_specs = (
        P(None, "tp", "seq"),
        P(None, "tp", None),
        P(None, "tp", None),
        P("tp", None),
        P("tp", None),
        P("tp"),
        P(None, "tp"),
    )
    out_specs = P("tp", "seq")
    return jax.shard_map(
        per_device, mesh=mesh, in_specs=in_specs, out_specs=out_specs, check_vma=False
    )
```

profile of v0, /device:TPU:1, one launch (start us, length us, event | category | flops | bytes accessed | tf_op | source)
XLA Modules:
  0.0 517.9 jit_solution(7962565166536409826)
XLA Ops:
  6.5 3.2 copy.38
  10.6 4.0 collective-permute-start
  15.7 6.2 %fusion.8 = f32[3,512,256]{1,2,0:T(8,128)S(1)} fusion(f32[3,512,6]{1,2,0:T(8,128)S(1)} %collective-permute-done, f32[3,512,256]{1,2,0:T(8,128)} %copy.38, f32[3,512]{1,0:T(4,128)S(1)} %get-tuple-element.182, f32[3,512]{1,0:T(4,128)S(1)} %get-tuple-element.183, f32[3,512]{1,0:T(4,128)S(1)} %get-tuple-element.184, f32[3,512]{1,0:T(4,128)S(1)} %get-tuple-element.185, ...), kind=kLoop, calls=%fused_computation.22 | loop fusion | flops 7471104 | bytes 3225600 | tf_op jit(solution)/shard_map/add | solution.py:36
  22.0 1.2 copy-done.2
  23.1 1.0 slice.121
  24.1 3.7 collective-permute-start.1
  30.0 10.0 %collective-permute-done.1 = f32[3,512,127]{1,2,0:T(8,128)S(1)} collective-permute-done((f32[3,512,127]{1,2,0:T(8,128)}, f32[3,512,127]{1,2,0:T(8,128)S(1)}, u32[]{:S(2)}, u32[]{:S(2)}) %collective-permute-start.1) | collective-permute-done | bytes 780320 | tf_op jit(solution)/shard_map/ppermute | solution.py:14
  40.0 3.2 pad_maximum_fusion.1
  43.2 76.7 %while.24 = (s32[]{:T(128)}, f32[3,512,256]{2,1,0:T(8,128)}, f32[3,512,383]{1,2,0:T(8,128)}, f32[3,32,128]{2,1,0:T(8,128)}, s32[]{:T(128)}, /*index=5*/f32[]{:T(128)}) while((s32[]{:T(128)}, f32[3,512,256]{2,1,0:T(8,128)}, f32[3,512,383]{1,2,0:T(8,128)}, f32[3,32,128]{2,1,0:T(8,128)}, s32[]{:T(128)}, /*index=5*/f32[]{:T(128)}) %tuple.62), condition=%wide.region_1.2_spmd, body=%wide.region_0.1_spmd.sunk | while | flops 401341440 | bytes 51931760 | solution.py:95
  43.2 1.2 dynamic-slice_bitcast_fusion.7
  44.8 1.3 copy.99
  47.2 2.4 copy.98
  49.7 2.3 slice.204
  52.0 9.5 %reshape.103 = f32[32,128,255,1]{2,1,0,3:T(8,128)} reshape(f32[32,32640]{1,0:T(8,128)} %slice.204) | data formatting | bytes 8355840 | tf_op jit(solution)/shard_map/while/body/eval_jaxpr/vmap()/reshape | solution.py:43
  61.4 5.8 %fusion.65 = f32[32,16,2,128]{3,1,2,0:T(8,128)S(1)} fusion(f32[32,128,255,1]{2,1,0,3:T(8,128)} %reshape.103, f32[32,16,2,255]{3,1,0,2:T(8,128)S(1)} %bitcast.117), kind=kOutput, calls=%fused_computation.clone.1 | convolution fusion | flops 401080320 | bytes 5746688 | tf_op jit(solution)/shard_map/while/body/eval_jaxpr/gcbs,gts->gcbt/dot_general | solution.py:60
  68.8 1.2 dynamic-slice_bitcast_fusion.7
  70.4 1.3 copy.99
  72.8 2.4 copy.98
  75.3 2.3 slice.204
  77.6 9.5 %reshape.103 = f32[32,128,255,1]{2,1,0,3:T(8,128)} reshape(f32[32,32640]{1,0:T(8,128)} %slice.204) | data formatting | bytes 8355840 | tf_op jit(solution)/shard_map/while/body/eval_jaxpr/vmap()/reshape | solution.py:43
  87.0 5.8 %fusion.65 = f32[32,16,2,128]{3,1,2,0:T(8,128)S(1)} fusion(f32[32,128,255,1]{2,1,0,3:T(8,128)} %reshape.103, f32[32,16,2,255]{3,1,0,2:T(8,128)S(1)} %bitcast.117), kind=kOutput, calls=%fused_computation.clone.1 | convolution fusion | flops 401080320 | bytes 5746688 | tf_op jit(solution)/shard_map/while/body/eval_jaxpr/gcbs,gts->gcbt/dot_general | solution.py:60
  94.4 1.2 dynamic-slice_bitcast_fusion.7
  96.0 1.3 copy.99
  98.4 2.4 copy.98
  100.8 2.3 slice.204
  103.1 9.5 %reshape.103 = f32[32,128,255,1]{2,1,0,3:T(8,128)} reshape(f32[32,32640]{1,0:T(8,128)} %slice.204) | data formatting | bytes 8355840 | tf_op jit(solution)/shard_map/while/body/eval_jaxpr/vmap()/reshape | solution.py:43
  112.6 5.8 %fusion.65 = f32[32,16,2,128]{3,1,2,0:T(8,128)S(1)} fusion(f32[32,128,255,1]{2,1,0,3:T(8,128)} %reshape.103, f32[32,16,2,255]{3,1,0,2:T(8,128)S(1)} %bitcast.117), kind=kOutput, calls=%fused_computation.clone.1 | convolution fusion | flops 401080320 | bytes 5746688 | tf_op jit(solution)/shard_map/while/body/eval_jaxpr/gcbs,gts->gcbt/dot_general | solution.py:60
  120.0 1.3 slice_multiply_fusion
  121.5 1.4 fusion.30
  122.9 2.0 copy.45
  124.9 4.6 fusion.51
  130.5 1.4 copy.51
  132.6 1.1 fusion.46
  134.3 2.4 copy.73
  136.8 2.2 slice.124
  139.0 9.4 %reshape.86 = f32[32,128,255]{2,1,0:T(8,128)} reshape(f32[32,32640]{1,0:T(8,128)} %slice.124) | data formatting | bytes 8355840 | tf_op jit(solution)/shard_map/vmap()/reshape | solution.py:69
  148.4 101.7 %all-gather.2 = f32[64,32,16]{1,2,0:T(8,128)} all-gather(f32[1,32,16]{1,2,0:T(8,128)S(1)} %copy-done.7), channel_id=2, replica_groups=mesh['seq'=64,'tp'=8] {'seq'}, dimensions={0}, use_global_device_ids=true | all-gather | bytes 133120 | tf_op jit(solution)/shard_map/all_gather | solution.py:19
  252.7 85.9 %all-gather.5.cloned.1.call-done = f32[2048,16,16]{2,1,0:T(8,128)} async-done(((f32[32,16,16]{2,1,0:T(8,128)}), f32[2048,16,16]{2,1,0:T(8,128)}) %all-gather.5.cloned.1.call-update) | async-done | bytes 2097168 | tf_op jit(solution)/shard_map/all_gather | solution.py:19
  338.7 13.4 %copy.48 = f32[64,32,16,16]{1,3,2,0:T(8,128)} copy(f32[64,32,16,16]{3,2,1,0:T(8,128)} %bitcast.118) | data formatting | bytes 4194304
  352.0 107.0 %while.25 = (s32[]{:T(128)}, f32[32,16,16]{0,2,1:T(8,128)S(1)}, s32[]{:T(128)}, f32[64,32,16]{1,2,0:T(8,128)}, f32[64,32,16,16]{1,3,2,0:T(8,128)}, /*index=5*/s32[]{:T(128)}, s32[]{:T(128)}) while((s32[]{:T(128)}, f32[32,16,16]{0,2,1:T(8,128)S(1)}, s32[]{:T(128)}, f32[64,32,16]{1,2,0:T(8,128)}, f32[64,32,16,16]{1,3,2,0:T(8,128)}, ...), condition=%wide.region_3.4_spmd.clone, body=%wide.region_2.3_spmd.clone.sunk | while | flops 32772 | bytes 104553 | solution.py:28
  352.7 1.0 fusion.66
  356.1 1.0 fusion.66
  459.3 5.3 %fusion.23 = f32[32,16,2,16]{1,2,3,0:T(2,128)S(1)} fusion(f32[32,16,2,16]{1,2,3,0:T(2,128)} %copy.45, pred[2,2]{1,0:T(4,128)(4,1)} %fusion.47, f32[32,2,16]{1,2,0:T(8,128)} %multiply_exponential_fusion, f32[32,16,16]{1,2,0:T(8,128)S(1)} %copy.49, f32[2,2]{1,0:T(2,128)} %maximum_convert_fusion, f32[32,16]{1,0:T(8,128)} %copy-done.4), kind=kOutput, calls=%fused_computation.42 | convolution fusion | flops 430080 | bytes 170004 | tf_op jit(solution)/shard_map/gnbe,gcen->gcbn/dot_general | solution.py:121
  464.6 1.1 fusion.26
  465.8 3.4 fusion.22
  469.5 3.3 convolution_bitcast_fusion
  472.9 36.4 %reduce-scatter.2.cloned.1.call-done = f32[256,256]{0,1:T(8,128)} async-done(((f32[2048,256]{0,1:T(8,128)}), f32[256,256]{0,1:T(8,128)}) %reduce-scatter.2.cloned.1.call-update) | async-done | bytes 262160 | tf_op jit(solution)/shard_map/reduce_scatter | solution.py:127
  509.3 1.8 copy.54
  (224 shorter events, 122.8 us)
Async XLA Ops:
  6.5 463.0 %copy-start = (bf16[2048,512]{1,0:T(8,128)(2,1)S(1)}, bf16[2048,512]{1,0:T(8,128)(2,1)}, u32[]{:S(2)}) copy-start(bf16[2048,512]{1,0:T(8,128)(2,1)} %param.17) | copy-start | bytes 6291460
  6.5 8.0 %copy-start.8 = (f32[3,32,7]{1,2,0:T(8,128)S(1)}, f32[3,32,7]{1,2,0:T(8,128)}, u32[]{:S(2)}) copy-start(f32[3,32,7]{1,2,0:T(8,128)} %param.12) | copy-start | bytes 8068
  6.5 332.1 %all-gather.5.cloned.1.call-start = ((), (), s32[]{:S(2)}) async-start(), calls=%async_computation.2 | async-start | bytes 17039360 | tf_op jit(solution)/shard_map/all_gather | solution.py:19
  10.6 5.2 collective-permute-start
  22.0 1.2 copy-start.2
  23.1 4.7 copy-start.9
  23.1 4.7 copy-start.10
  24.1 15.9 %collective-permute-start.1 = (f32[3,512,127]{1,2,0:T(8,128)}, f32[3,512,127]{1,2,0:T(8,128)S(1)}, u32[]{:S(2)}, u32[]{:S(2)}) collective-permute-start(f32[3,512,127]{1,2,0:T(8,128)} %slice.121), channel_id=1, source_target_pairs={{0,8},{8,16},{16,24},{24,32},{32,40},{40,48},{48,56},{56,64},{64,7... | collective-permute-start | bytes 2340872 | tf_op jit(solution)/shard_map/ppermute | solution.py:14
  28.6 0.5 copy-start.12
  29.2 14.1 %copy-start.4 = (f32[32,16]{1,0:T(8,128)}, f32[32,16]{1,0:T(8,128)S(1)}, u32[]{:S(2)}) copy-start(f32[32,16]{1,0:T(8,128)S(1)} %copy.44) | copy-start | bytes 6148
  52.0 9.5 %copy-start.1 = (f32[512,2,255]{2,0,1:T(8,128)S(1)}, f32[512,2,255]{2,0,1:T(8,128)}, u32[]{:S(2)}) copy-start(f32[512,2,255]{2,0,1:T(8,128)} %copy.99) | copy-start | bytes 3133444 | tf_op jit(solution)/shard_map/while
  77.6 9.5 %copy-start.1 = (f32[512,2,255]{2,0,1:T(8,128)S(1)}, f32[512,2,255]{2,0,1:T(8,128)}, u32[]{:S(2)}) copy-start(f32[512,2,255]{2,0,1:T(8,128)} %copy.99) | copy-start | bytes 3133444 | tf_op jit(solution)/shard_map/while
  103.1 9.5 %copy-start.1 = (f32[512,2,255]{2,0,1:T(8,128)S(1)}, f32[512,2,255]{2,0,1:T(8,128)}, u32[]{:S(2)}) copy-start(f32[512,2,255]{2,0,1:T(8,128)} %copy.99) | copy-start | bytes 3133444 | tf_op jit(solution)/shard_map/while
  130.4 378.9 %reduce-scatter.2.cloned.1.call-start = ((), (), s32[]{:S(2)}) async-start(), calls=%async_computation.1 | async-start | bytes 2359296 | tf_op jit(solution)/shard_map/reduce_scatter | solution.py:127
  139.0 9.5 %copy-start.7 = (f32[1,32,16]{1,2,0:T(8,128)S(1)}, f32[1,32,16]{1,2,0:T(8,128)}, u32[]{:S(2)}) copy-start(f32[1,32,16]{1,2,0:T(8,128)} %get-tuple-element.180) | copy-start | bytes 6148
  139.0 112.9 %copy-start.5 = (f32[32,16]{1,0:T(8,128)S(1)}, f32[32,16]{1,0:T(8,128)}, u32[]{:S(2)}) copy-start(f32[32,16]{1,0:T(8,128)} %copy-done.4) | copy-start | bytes 6148
  459.3 5.3 %copy-start.6 = (f32[32,16]{1,0:T(8,128)S(1)}, f32[32,16]{1,0:T(8,128)}, u32[]{:S(2)}) copy-start(f32[32,16]{1,0:T(8,128)} %copy.51) | copy-start | bytes 6148
  459.3 5.3 %copy-start.13 = (f32[128]{0:T(128)S(1)}, f32[128]{0:T(128)}, u32[]{:S(2)}) copy-start(f32[128]{0:T(128)} %broadcast_add_fusion) | copy-start | bytes 1540
  459.3 6.5 %copy-start.3 = (f32[32,128,255]{2,1,0:T(8,128)S(1)}, f32[32,128,255]{2,1,0:T(8,128)}, u32[]{:S(2)}) copy-start(f32[32,128,255]{2,1,0:T(8,128)} %reshape.86) | copy-start | bytes 12533764
  465.8 3.7 copy-start.11
Sparse Core Ops, SparseCore 0:
  130.5 208.0 all-gather.4
  473.0 36.2 reduce-scatter.1
where the time goes:
time: 523 us; the launch traced here: 518 us
  local copies, waits for them, and re-layouts  146 us (28%)
  waiting for transfers between devices  133 us (25%)
  blocking collectives  102 us (20%)
  other arithmetic  77.2 us (15%)
  matrix products  37.6 us (7%)
  between operations  13.7 us (3%)
  starting transfers between devices  7.76 us (1%)
    all_gather x1, blocking collectives, prefix_2(): pieces = jax.tree.map(lambda part: lax.all_gather(part, axis), value)  102 us
    all_gather x1, waiting for transfers between devices, prefix_2(): pieces = jax.tree.map(lambda part: lax.all_gather(part, axis), value)  85.9 us
    select_n x63, other arithmetic, lap(): jnp.where(position < mine, new, old)  61.8 us
    mul x63, local copies, waits for them, and re-layouts, combine_states(): before[1] * behind[0][:, None, :] + behind[1]  44.2 us
    reduce_scatter x1, waiting for transfers between devices, per_device(): lax.psum_scatter(jnp.dot(out_weight, gated_out, preferred_element_type=jn...  36.4 us
    reshape x3, local copies, waits for them, and re-layouts, medium_matrix(): jnp.tile(pattern, block_len)[:block_len * (2 * block_len - 1)]  28.4 us
    unnamed x33, local copies, waits for them, and re-layouts  20.5 us
    dot_general x3, matrix products, medium_branch(): jnp.einsum('gcbs,gts->gcbt', windows, matrices, precision=lax.Precision.H...  17.4 us
  transfers between devices with their start and end apart: 4, of which 4 were waited for; matrix products, arithmetic and copies ran while one was open for 4% of the time, Pallas kernels for 0%

commit v1 on v0

v1 whole, which is shorter than its diff:
```python
import functools

import jax
import jax.numpy as jnp
from jax import lax
from jax.experimental import pallas as pl
from jax.experimental.pallas import tpu as pltpu
from jax.sharding import PartitionSpec as P

GROUP = 16
SHORT = 7
MEDIUM = 128
ORDER = 16
LANES = 128


def split(x):
    high = x.astype(jnp.bfloat16)
    return high, (x - high.astype(jnp.float32)).astype(jnp.bfloat16)


def dot_split(left, right, dims):
    a_high, a_low = left
    b_high, b_low = right
    one = functools.partial(
        lax.dot_general, dimension_numbers=(dims, ((), ())), preferred_element_type=jnp.float32
    )
    return one(a_high, b_high) + (one(a_high, b_low) + one(a_low, b_high))


NN = ((1,), (0,))
NT = ((1,), (1,))


def iota(shape, axis):
    return lax.broadcasted_iota(jnp.int32, shape, axis)


def filter_tables(short_ref, medium_ref, taps_ref):
    medium = medium_ref[...]
    wide = jnp.concatenate([medium, jnp.zeros_like(medium)], axis=1)
    short = short_ref[...]
    total = short[:, 0:1] * wide
    for j in range(1, SHORT):
        total = total + short[:, j : j + 1] * pltpu.roll(wide, j, 1)
    taps_ref[...] = total


def modal_tables(rates_ref, weight_ref, rate_rows_ref, weight_rows_ref, kernel_ref, ending_ref, readout_ref):
    length = kernel_ref.shape[1]
    steps = iota((1, length), 1).astype(jnp.float32)
    rates, weight = rates_ref[...], weight_ref[...]
    total = weight[:, 0:1] * jnp.exp(-rates[:, 0:1] * steps)
    for n in range(1, ORDER):
        total = total + weight[:, n : n + 1] * jnp.exp(-rates[:, n : n + 1] * steps)
    kernel_ref[...] = total
    rate_rows = rate_rows_ref[...]
    ending_ref[...] = jnp.exp(-rate_rows * (length - 1.0 - steps))
    readout_ref[...] = weight_rows_ref[...] * jnp.exp(-rate_rows * (steps + 1.0))


def toeplitz(row, rows):
    return pltpu.roll(jnp.broadcast_to(row, (rows, row.shape[1])), 0, 1, stride=1, stride_axis=0)


def filter_group(extra, halo, own, taps_row):
    rolled = toeplitz(taps_row, LANES)
    near, middle = rolled[:, :LANES], rolled[:, LANES:]
    causal = iota((LANES, LANES), 1) >= iota((LANES, LANES), 0)
    matrix = jnp.concatenate(
        [jnp.where(causal, 0.0, near), middle, jnp.where(causal, near, 0.0)], axis=0
    )
    tiles = [extra, halo, own[:, :LANES], own[:, LANES:]]
    windows = jnp.concatenate(
        [jnp.concatenate(tiles[0:3], axis=1), jnp.concatenate(tiles[1:4], axis=1)], axis=0
    )
    result = dot_split(split(windows), split(matrix), NN)
    return jnp.concatenate([result[:GROUP], result[GROUP:]], axis=1)


def mix_kernel(
    features_ref, halo_ref, extra_ref, short_ref, medium_ref, rates_ref, weight_ref,
    rate_rows_ref, weight_rows_ref, gain_ref,
    query_ref, base_ref, state_ref, readout_ref,
    taps_ref, kernel_ref, ending_ref, product_ref,
):
    groups, length = kernel_ref.shape
    filter_tables(short_ref, medium_ref, taps_ref)
    modal_tables(rates_ref, weight_ref, rate_rows_ref, weight_rows_ref, kernel_ref, ending_ref, readout_ref)

    def group_step(g, carry):
        rows = pl.ds(pl.multiple_of(g * GROUP, GROUP), GROUP)
        done = [
            filter_group(
                extra_ref[i, rows, :], halo_ref[i, rows, :], features_ref[i, rows, :],
                taps_ref[pl.ds(i * groups + g, 1), :],
            )
            for i in range(3)
        ]
        product = done[1] * done[2]
        query_ref[rows, :] = done[0]
        product_ref[rows, :] = product
        rolled = toeplitz(kernel_ref[pl.ds(g, 1), :], length)
        causal = iota((length, length), 1) >= iota((length, length), 0)
        inside = dot_split(split(product), split(jnp.where(causal, rolled, 0.0)), NN)
        base_ref[rows, :] = inside + gain_ref[rows, :] * product
        return carry

    lax.fori_loop(0, groups, group_step, 0)
    same = iota((LANES, LANES), 0) // ORDER == iota((LANES, LANES), 1) // GROUP
    for block in range(product_ref.shape[0] // LANES):
        rows = slice(block * LANES, (block + 1) * LANES)
        full = dot_split(split(ending_ref[rows, :]), split(product_ref[rows, :]), NT)
        full = jnp.where(same, full, 0.0)
        total = full[0:ORDER]
        for k in range(1, LANES // ORDER):
            total = total + full[k * ORDER : (k + 1) * ORDER]
        state_ref[:, rows] = total


def finish_kernel(query_ref, base_ref, incoming_ref, readout_ref, weight_ref, out_ref, gated_ref):
    same = iota((LANES, LANES), 1) // ORDER == iota((LANES, LANES), 0) // GROUP
    for block in range(query_ref.shape[0] // LANES):
        rows = slice(block * LANES, (block + 1) * LANES)
        across = jnp.transpose(incoming_ref[:, rows])
        spread = jnp.where(same, jnp.concatenate([across] * (LANES // ORDER), axis=1), 0.0)
        carried = dot_split(split(spread), split(readout_ref[rows, :]), NN)
        gated_ref[rows, :] = (query_ref[rows, :] * (base_ref[rows, :] + carried)).astype(jnp.bfloat16)
    gated = gated_ref[...]
    step = 256

    def rows_step(k, carry):
        rows = pl.ds(pl.multiple_of(k * step, step), step)
        out_ref[rows, :] = jnp.dot(weight_ref[rows, :], gated, preferred_element_type=jnp.float32)
        return carry

    lax.fori_loop(0, out_ref.shape[0] // step, rows_step, 0)


def passed_along(block, axis):
    devices = lax.axis_size(axis)
    return lax.ppermute(block, axis, [(i, i + 1) for i in range(devices - 1)])


def vmem():
    return pl.BlockSpec(memory_space=pltpu.VMEM)


def per_device(features, short_filter, medium_filter, rates, residues, skip_gain, out_weight):
    channels, length = features.shape[1:]
    groups = rates.shape[0]
    f32 = jnp.float32
    halo = passed_along(features[:, :, length - LANES :], "seq")
    extra = passed_along(features[:, :, length - LANES - 8 : length - LANES], "seq")
    extra = jnp.pad(extra, ((0, 0), (0, 0), (LANES - 8, 0)))
    weight = residues * jnp.sqrt(-jnp.expm1(-2.0 * rates))
    query, base, state, readout = pl.pallas_call(
        mix_kernel,
        out_shape=(
            jax.ShapeDtypeStruct((channels, length), f32),
            jax.ShapeDtypeStruct((channels, length), f32),
            jax.ShapeDtypeStruct((ORDER, channels), f32),
            jax.ShapeDtypeStruct((groups * ORDER, length), f32),
        ),
        in_specs=[vmem()] * 10,
        out_specs=(vmem(),) * 4,
        scratch_shapes=[
            pltpu.VMEM((3 * groups, length), f32),
            pltpu.VMEM((groups, length), f32),
            pltpu.VMEM((groups * ORDER, length), f32),
            pltpu.VMEM((channels, length), f32),
        ],
        compiler_params=pltpu.CompilerParams(vmem_limit_bytes=48 * 1024 * 1024),
    )(
        features, halo, extra, short_filter.reshape(3 * groups, SHORT), medium_filter.reshape(3 * groups, MEDIUM),
        rates, weight, rates.reshape(-1, 1), weight.reshape(-1, 1), skip_gain[:, None],
    )
    gathered = lax.all_gather(state, "seq")
    count, mine = lax.axis_size("seq"), lax.axis_index("seq")
    place = jnp.arange(count)
    gap = jnp.maximum(mine - 1 - place, 0).astype(f32)
    rates_wide = jnp.repeat(rates.T, GROUP, axis=1)
    decay = jnp.exp(-rates_wide[None] * (length * gap)[:, None, None])
    incoming = jnp.sum(jnp.where((place < mine)[:, None, None], decay * gathered, 0.0), axis=0)
    partial = pl.pallas_call(
        finish_kernel,
        out_shape=jax.ShapeDtypeStruct((out_weight.shape[0], length), f32),
        in_specs=[vmem()] * 5,
        out_specs=vmem(),
        scratch_shapes=[pltpu.VMEM((channels, length), jnp.bfloat16)],
        compiler_params=pltpu.CompilerParams(vmem_limit_bytes=48 * 1024 * 1024),
    )(query, base, incoming, readout, out_weight)
    return lax.psum_scatter(partial, "tp", scatter_dimension=0, tiled=True)


def solution(mesh):
    in_specs = (
        P(None, "tp", "seq"),
        P(None, "tp", None),
        P(None, "tp", None),
        P("tp", None),
        P("tp", None),
        P("tp"),
        P(None, "tp"),
    )
    out_specs = P("tp", "seq")
    return jax.shard_map(
        per_device, mesh=mesh, in_specs=in_specs, out_specs=out_specs, check_vma=False
    )
```

time: 523 us -> 255 us (0.49)
  local copies, waits for them, and re-layouts: 146 us -> 10.8 us
  blocking collectives: 102 us -> 0 us
  other arithmetic: 77.2 us -> 2.13 us
  waiting for transfers between devices: 133 us -> 197 us
  matrix products: 37.6 us -> 0 us
  Pallas kernels: 0 us -> 23.6 us
    all_gather x1 -> x0, blocking collectives: 102 us -> none  [prefix_2(): pieces = jax.tree.map(lambda part: lax.all_gather(part, axis), value)]
    select_n x63 -> x0, other arithmetic: 61.8 us -> none  [lap(): jnp.where(position < mine, new, old)]
    all_gather x1, waiting for transfers between devices: 85.9 us -> 141 us  [per_device(): gathered = lax.all_gather(state, 'seq')]
    mul x67 -> x0, local copies, waits for them, and re-layouts: 46.7 us -> none  [the longest x63 44.2 us: combine_states(): before[1] * behind[0][:, None, :] + behind[1]]
    reshape x5 -> x2, local copies, waits for them, and re-layouts: 38.1 us -> 0.31 us  [the longest x1 0.16 us: per_device(): weight.reshape(-1, 1)]
    dot_general x10 -> x0, matrix products: 37.6 us -> none  [the longest x3 17.4 us: medium_branch(): jnp.einsum('gcbs,gts->gcbt', windows, matrices, precision=lax.Precision.H...]
    pallas_call x0 -> x2, Pallas kernels: none -> 23.6 us  [the longest x1 19.5 us: per_device(): pl.pallas_call(mix_kernel, out_shape=(jax.ShapeDtypeStruct((channels, len...]
    unnamed x33 -> x30, local copies, waits for them, and re-layouts: 20.5 us -> 5 us
  transfers between devices with their start and end apart: 4 -> 4, of which waited for: 4 -> 3; matrix products, arithmetic and copies ran while one was open for 4% -> 2% of each run, Pallas kernels for 0% -> 0%
where the time goes in v1:
time: 255 us; the launch traced here: 254 us
  waiting for transfers between devices  197 us (77%)
  Pallas kernels  23.6 us (9%)
  between operations  13.6 us (5%)
  local copies, waits for them, and re-layouts  10.8 us (4%)
  starting transfers between devices  7.29 us (3%)
    all_gather x1, waiting for transfers between devices, per_device(): gathered = lax.all_gather(state, 'seq')  141 us
    reduce_scatter x1, waiting for transfers between devices, per_device(): return lax.psum_scatter(partial, 'tp', scatter_dimension=0, tiled=True)  45.8 us
    pallas_call x1, Pallas kernels, per_device(): pl.pallas_call(mix_kernel, out_shape=(jax.ShapeDtypeStruct((channels, len...  19.5 us
    ppermute x2, waiting for transfers between devices, passed_along(): return lax.ppermute(block, axis, [(i, i + 1) for i in range(devices - 1)])  9.79 us
    ppermute x2, starting transfers between devices, passed_along(): return lax.ppermute(block, axis, [(i, i + 1) for i in range(devices - 1)])  7.21 us
  transfers between devices with their start and end apart: 4, of which 3 were waited for; matrix products, arithmetic and copies ran while one was open for 2% of the time, Pallas kernels for 0%

profile of v1, /device:TPU:1, one launch (start us, length us, event | category | flops | bytes accessed | tf_op | source)
XLA Modules:
  0.0 254.0 jit_solution(12248341508587221031)
XLA Ops:
  6.5 0.0 copy-start
  6.5 0.0 copy-start.9
  6.5 0.0 copy-start.11
  6.5 0.0 copy-start.12
  6.5 0.0 copy-start.10
  6.5 0.0 all-gather.3.cloned.1.call-start
  6.6 2.2 slice.6
  8.8 4.1 %collective-permute-start = (f32[3,512,128]{2,1,0:T(8,128)}, f32[3,512,128]{2,1,0:T(8,128)S(1)}, u32[]{:S(2)}, u32[]{:S(2)}) collective-permute-start(f32[3,512,128]{2,1,0:T(8,128)} %slice.6), channel_id=1, source_target_pairs={{0,8},{8,16},{16,24},{24,32},{32,40},{40,48},{48,56},{56,64},{64,7... | collective-permute-start | bytes 2359304 | tf_op jit(solution)/shard_map/ppermute | solution.py:142
  12.9 0.0 copy-done
  12.9 0.3 slice.7
  13.1 0.0 copy-start.8
  13.1 0.2 copy.42
  13.4 3.2 %collective-permute-start.1 = (f32[3,512,8]{1,2,0:T(8,128)S(1)}, f32[3,512,8]{1,2,0:T(8,128)S(1)}, u32[]{:S(2)}, u32[]{:S(2)}) collective-permute-start(f32[3,512,8]{1,2,0:T(8,128)S(1)} %copy.42), channel_id=1, source_target_pairs={{0,8},{8,16},{16,24},{24,32},{32,40},{40,48},{48,56},{56,64},{64,7... | collective-permute-start | bytes 147464 | tf_op jit(solution)/shard_map/ppermute | solution.py:142
  16.5 0.0 copy-done.9
  16.5 0.1 copy.38.rates_ref
  16.6 0.0 copy-done.11
  16.6 0.1 copy.36
  16.7 0.2 reshape.36.rate_rows_ref
  16.9 0.2 reshape.37.weight_rows_ref
  17.1 0.0 copy-done.12
  17.1 0.1 copy.41.gain_ref
  17.2 0.0 copy-done.10
  17.2 0.1 copy.33
  17.3 9.8 %collective-permute-done.1 = f32[3,512,8]{1,2,0:T(8,128)S(1)} collective-permute-done((f32[3,512,8]{1,2,0:T(8,128)S(1)}, f32[3,512,8]{1,2,0:T(8,128)S(1)}, u32[]{:S(2)}, u32[]{:S(2)}) %collective-permute-start.1) | collective-permute-done | bytes 49184 | tf_op jit(solution)/shard_map/ppermute | solution.py:142
  27.1 1.2 copy.32
  28.3 1.4 pad.4.extra_ref
  29.7 0.0 collective-permute-done.halo_ref
  29.7 0.0 copy-done.8
  29.7 19.5 %shard_map.73 = (f32[512,256]{1,0:T(8,128)S(1)}, f32[512,256]{1,0:T(8,128)S(1)}, f32[16,512]{1,0:T(8,128)}, f32[512,256]{1,0:T(8,128)S(1)}) custom-call(f32[3,512,256]{2,1,0:T(8,128)S(1)} %copy-done, f32[3,512,128]{2,1,0:T(8,128)S(1)} %collective-permute-done.halo_ref, f32[3,512,128]{2,1,0:T(8,128)S(1)} %pad.4.extra_ref, f32[96,7]{1,0:T(8,128)S(1)} %bitcast.6, ...), custom_call_target="tpu_custom_call" | custom-call | tf_op jit(solution)/shard_map/pallas_call | solution.py:157
  49.2 0.0 copy-start.2
  49.2 0.8 copy-done.2
  50.1 0.0 copy-start.4
  50.1 0.8 copy-done.4
  50.9 0.8 copy-done.6
  51.7 0.0 all-gather.3.cloned.1.call-update
  51.7 0.0 reduce-scatter.2.cloned.1.call-start
  51.8 0.1 broadcast_in_dim.22
  51.9 0.2 neg.21
  52.1 141.0 %all-gather.3.cloned.1.call-done = f32[1024,512]{1,0:T(8,128)} async-done(((f32[16,512]{1,0:T(8,128)}), f32[1024,512]{1,0:T(8,128)}) %all-gather.3.cloned.1.call-update) | async-done | bytes 2097168 | tf_op jit(solution)/shard_map/all_gather | solution.py:178
  193.1 2.1 select_reduce_fusion.incoming_ref
  195.2 0.0 copy-done.1
  195.2 0.0 copy-done.3
  195.2 0.0 copy-start.5
  195.2 1.0 copy-done.5
  196.3 1.0 copy-done.7
  197.3 4.1 %shard_map.74 = f32[2048,256]{1,0:T(8,128)} custom-call(f32[512,256]{1,0:T(8,128)S(1)} %copy-done.3, f32[512,256]{1,0:T(8,128)S(1)} %copy-done.5, f32[16,512]{1,0:T(8,128)S(1)} %select_reduce_fusion.incoming_ref, f32[512,256]{1,0:T(8,128)S(1)} %copy-done.7, bf16[2048,512]{1,0:T(8,128)(2,1)S(1)} %copy-done.1), custom_call_target="tpu_custom_call" | custom-call | tf_op jit(solution)/shard_map/pallas_call | solution.py:185
  201.4 0.0 reduce-scatter.2.cloned.1.call-update
  201.4 45.8 %reduce-scatter.2.cloned.1.call-done = f32[256,256]{1,0:T(8,128)} async-done(((f32[2048,256]{1,0:T(8,128)}), f32[256,256]{1,0:T(8,128)}) %reduce-scatter.2.cloned.1.call-update) | async-done | bytes 262160 | tf_op jit(solution)/shard_map/reduce_scatter | solution.py:193
  (8 shorter events, 0.0 us)
Async XLA Ops:
  6.5 6.3 %copy-start = (f32[3,512,256]{2,1,0:T(8,128)S(1)}, f32[3,512,256]{2,1,0:T(8,128)}, u32[]{:S(2)}) copy-start(f32[3,512,256]{2,1,0:T(8,128)} %features_ref.1) | copy-start | bytes 4718596
  6.5 10.0 %copy-start.9 = (f32[32,16]{0,1:T(8,128)S(1)}, f32[32,16]{0,1:T(8,128)}, u32[]{:S(2)}) copy-start(f32[32,16]{0,1:T(8,128)} %param.10) | copy-start | bytes 6148
  6.5 10.1 %copy-start.11 = (f32[32,16]{0,1:T(8,128)S(1)}, f32[32,16]{0,1:T(8,128)}, u32[]{:S(2)}) copy-start(f32[32,16]{0,1:T(8,128)} %param.11) | copy-start | bytes 6148
  6.5 10.5 %copy-start.12 = (f32[512]{0:T(512)S(1)}, f32[512]{0:T(512)}, u32[]{:S(2)}) copy-start(f32[512]{0:T(512)} %param.12) | copy-start | bytes 6148
  6.5 10.7 %copy-start.10 = (f32[3,32,7]{1,2,0:T(8,128)S(1)}, f32[3,32,7]{1,2,0:T(8,128)}, u32[]{:S(2)}) copy-start(f32[3,32,7]{1,2,0:T(8,128)} %param.8) | copy-start | bytes 8068
  6.5 186.5 %all-gather.3.cloned.1.call-start = ((), (), s32[]{:S(2)}) async-start(), calls=%async_computation.2 | async-start | bytes 2129920 | tf_op jit(solution)/shard_map/all_gather | solution.py:178
  8.8 20.9 %collective-permute-start = (f32[3,512,128]{2,1,0:T(8,128)}, f32[3,512,128]{2,1,0:T(8,128)S(1)}, u32[]{:S(2)}, u32[]{:S(2)}) collective-permute-start(f32[3,512,128]{2,1,0:T(8,128)} %slice.6), channel_id=1, source_target_pairs={{0,8},{8,16},{16,24},{24,32},{32,40},{40,48},{48,56},{56,64},{64,7... | collective-permute-start | bytes 2359304 | tf_op jit(solution)/shard_map/ppermute | solution.py:142
  13.1 16.6 %copy-start.8 = (f32[3,32,128]{2,1,0:T(8,128)S(1)}, f32[3,32,128]{2,1,0:T(8,128)}, u32[]{:S(2)}) copy-start(f32[3,32,128]{2,1,0:T(8,128)} %param.9) | copy-start | bytes 147460
  13.4 13.8 %collective-permute-start.1 = (f32[3,512,8]{1,2,0:T(8,128)S(1)}, f32[3,512,8]{1,2,0:T(8,128)S(1)}, u32[]{:S(2)}, u32[]{:S(2)}) collective-permute-start(f32[3,512,8]{1,2,0:T(8,128)S(1)} %copy.42), channel_id=1, source_target_pairs={{0,8},{8,16},{16,24},{24,32},{32,40},{40,48},{48,56},{56,64},{64,7... | collective-permute-start | bytes 147464 | tf_op jit(solution)/shard_map/ppermute | solution.py:142
  49.2 0.8 copy-start.2
  50.1 0.8 copy-start.4
  50.9 0.8 copy-start.6
  51.7 143.5 %copy-start.1 = (bf16[2048,512]{1,0:T(8,128)(2,1)S(1)}, bf16[2048,512]{1,0:T(8,128)(2,1)}, u32[]{:S(2)}) copy-start(bf16[2048,512]{1,0:T(8,128)(2,1)} %weight_ref.1) | copy-start | bytes 6291460
  51.7 143.5 %copy-start.3 = (f32[512,256]{1,0:T(8,128)S(1)}, f32[512,256]{1,0:T(8,128)}, u32[]{:S(2)}) copy-start(f32[512,256]{1,0:T(8,128)} %copy-done.2) | copy-start | bytes 1572868
  51.7 195.5 %reduce-scatter.2.cloned.1.call-start = ((), (), s32[]{:S(2)}) async-start(), calls=%async_computation.1 | async-start | bytes 2359296 | tf_op jit(solution)/shard_map/reduce_scatter | solution.py:193
  195.2 1.0 copy-start.5
  196.2 1.0 copy-start.7
Sparse Core Ops, SparseCore 0:
  51.8 141.2 all-gather.2
  201.5 45.6 reduce-scatter.1

commit v2 on v1

v2 whole, which is shorter than its diff:
```python
import functools

import jax
import jax.numpy as jnp
from jax import lax
from jax.experimental import pallas as pl
from jax.experimental.pallas import tpu as pltpu
from jax.sharding import PartitionSpec as P

GROUP = 16
SHORT = 7
MEDIUM = 128
ORDER = 16
LANES = 128
ROW = 4
RING = 4


def split(x):
    high = x.astype(jnp.bfloat16)
    return high, (x - high.astype(jnp.float32)).astype(jnp.bfloat16)


def dot_split(left, right, dims):
    a_high, a_low = left
    b_high, b_low = right
    one = functools.partial(
        lax.dot_general, dimension_numbers=(dims, ((), ())), preferred_element_type=jnp.float32
    )
    return one(a_high, b_high) + (one(a_high, b_low) + one(a_low, b_high))


NN = ((1,), (0,))
NT = ((1,), (1,))


def iota(shape, axis):
    return lax.broadcasted_iota(jnp.int32, shape, axis)


def filter_tables(short_ref, medium_ref, taps_ref):
    medium = medium_ref[...]
    wide = jnp.concatenate([medium, jnp.zeros_like(medium)], axis=1)
    short = short_ref[...]
    total = short[:, 0:1] * wide
    for j in range(1, SHORT):
        total = total + short[:, j : j + 1] * pltpu.roll(wide, j, 1)
    taps_ref[...] = total


def modal_tables(rates_ref, weight_ref, rate_rows_ref, weight_rows_ref, kernel_ref, ending_ref, readout_ref):
    length = kernel_ref.shape[1]
    steps = iota((1, length), 1).astype(jnp.float32)
    rates, weight = rates_ref[...], weight_ref[...]
    total = weight[:, 0:1] * jnp.exp(-rates[:, 0:1] * steps)
    for n in range(1, ORDER):
        total = total + weight[:, n : n + 1] * jnp.exp(-rates[:, n : n + 1] * steps)
    kernel_ref[...] = total
    rate_rows = rate_rows_ref[...]
    ending_ref[...] = jnp.exp(-rate_rows * (length - 1.0 - steps))
    readout_ref[...] = weight_rows_ref[...] * jnp.exp(-rate_rows * (steps + 1.0))


def toeplitz(row, rows):
    return pltpu.roll(jnp.broadcast_to(row, (rows, row.shape[1])), 0, 1, stride=1, stride_axis=0)


def filter_group(extra, halo, own, taps_row):
    rolled = toeplitz(taps_row, LANES)
    near, middle = rolled[:, :LANES], rolled[:, LANES:]
    causal = iota((LANES, LANES), 1) >= iota((LANES, LANES), 0)
    matrix = jnp.concatenate(
        [jnp.where(causal, 0.0, near), middle, jnp.where(causal, near, 0.0)], axis=0
    )
    tiles = [extra, halo, own[:, :LANES], own[:, LANES:]]
    windows = jnp.concatenate(
        [jnp.concatenate(tiles[0:3], axis=1), jnp.concatenate(tiles[1:4], axis=1)], axis=0
    )
    result = dot_split(split(windows), split(matrix), NN)
    return jnp.concatenate([result[:GROUP], result[GROUP:]], axis=1)


def wrapped(index, count):
    return lax.rem(index + count, count)


def layer_kernel(
    features_ref, short_ref, medium_ref, rates_ref, weight_ref, rate_rows_ref, weight_rows_ref,
    rate_blocks_ref, gain_ref, out_weight_ref,
    out_ref,
    halo_ref, packed_ref, extra_ref, taps_ref, kernel_ref, ending_ref, readout_ref,
    product_ref, query_ref, base_ref, gated_ref,
    state_ref, row_states_ref, total_ref, totals_ref, start_ref,
    given_ref, mine_ref, pair_ref, relay_ref, last_ref,
    halo_sems, row_sems, column_sems, start_sems, pair_sems, ring_sems,
):
    groups, length = kernel_ref.shape
    channels = product_ref.shape[0]
    blocks = channels // LANES
    count = lax.axis_size("seq")
    column = count // ROW
    seq, tp = lax.axis_index("seq"), lax.axis_index("tp")
    z, y = seq // ROW, lax.rem(seq, ROW)
    x, core = tp // 2, lax.rem(tp, 2)
    at_row = lambda k: (z * ROW + wrapped(y + k, ROW), tp)
    at_column = lambda k: (wrapped(z + k, column) * ROW + y, tp)
    at_ring = lambda k: (seq, wrapped(x + k, RING) * 2 + core)
    following, before = (wrapped(seq + 1, count), tp), (wrapped(seq - 1, count), tp)
    partner = (seq, x * 2 + 1 - core)

    def remote(source, target, sems, device):
        return pltpu.make_async_remote_copy(
            src_ref=source, dst_ref=target, send_sem=sems.at[0], recv_sem=sems.at[1],
            device_id=device, device_id_type=pl.DeviceIdType.MESH,
        )

    barrier = pltpu.get_barrier_semaphore()
    peers = [following, before, partner, at_ring(1), at_ring(-1)]
    peers += [at_row(k) for k in range(1, ROW)] + [at_column(k) for k in range(1, column)]
    for peer in peers:
        pl.semaphore_signal(barrier, inc=1, device_id=peer, device_id_type=pl.DeviceIdType.MESH)
    lane = iota((32, LANES), 1) // 8
    for i in range(3):
        packed = jnp.zeros((32, LANES), jnp.float32)
        for p in range(channels // 32):
            moved = pltpu.roll(features_ref[i, 32 * p : 32 * p + 32, 0:LANES], (8 * p + 8) % LANES, 1)
            packed = jnp.where(lane == p, moved, packed)
        packed_ref[i] = packed
    pl.semaphore_wait(barrier, len(peers))

    halo_copies = [
        remote(features_ref.at[i, :, pl.ds(length - LANES, LANES)], halo_ref.at[i], halo_sems.at[i], following)
        for i in range(3)
    ]
    extra_copy = remote(packed_ref, extra_ref, halo_sems.at[3], following)
    extra_copy.start()
    for i in (1, 2, 0):
        halo_copies[i].start()

    filter_tables(short_ref, medium_ref, taps_ref)
    modal_tables(rates_ref, weight_ref, rate_rows_ref, weight_rows_ref, kernel_ref, ending_ref, readout_ref)
    inner = seq > 0

    def branch(i, g):
        rows = pl.ds(pl.multiple_of(g * GROUP, GROUP), GROUP)
        packed = extra_ref[i, pl.ds(pl.multiple_of(lax.rem(g, 2) * GROUP, GROUP), GROUP), :]
        extra = pltpu.roll(packed, LANES - 8 - 8 * (g // 2), 1)
        zero = jnp.zeros((GROUP, LANES), jnp.float32)
        return filter_group(
            jnp.where(inner, extra, zero), jnp.where(inner, halo_ref[i, rows, :], zero),
            features_ref[i, rows, :], taps_ref[pl.ds(i * groups + g, 1), :],
        )

    def product_step(g, carry):
        rows = pl.ds(pl.multiple_of(g * GROUP, GROUP), GROUP)
        product = branch(1, g) * branch(2, g)
        product_ref[rows, :] = product
        rolled = toeplitz(kernel_ref[pl.ds(g, 1), :], length)
        causal = iota((length, length), 1) >= iota((length, length), 0)
        inside = dot_split(split(product), split(jnp.where(causal, rolled, 0.0)), NN)
        base_ref[rows, :] = inside + gain_ref[rows, :] * product
        return carry

    def query_step(g, carry):
        rows = pl.ds(pl.multiple_of(g * GROUP, GROUP), GROUP)
        query_ref[rows, :] = branch(0, g)
        return carry

    extra_copy.wait_recv()
    halo_copies[1].wait_recv()
    halo_copies[2].wait_recv()
    lax.fori_loop(0, groups, product_step, 0)

    same = iota((LANES, LANES), 0) // ORDER == iota((LANES, LANES), 1) // GROUP
    for b in range(blocks):
        rows = slice(b * LANES, (b + 1) * LANES)
        full = dot_split(split(ending_ref[rows, :]), split(product_ref[rows, :]), NT)
        full = jnp.where(same, full, 0.0)
        total = full[0:ORDER]
        for k in range(1, LANES // ORDER):
            total = total + full[k * ORDER : (k + 1) * ORDER]
        state_ref[b] = total
    row_copies = [
        remote(state_ref, row_states_ref.at[k - 1], row_sems.at[k - 1], at_row(k)) for k in range(1, ROW)
    ]
    for copy in row_copies:
        copy.start()

    halo_copies[0].wait_recv()
    lax.fori_loop(0, groups // 2, query_step, 0)

    for copy in row_copies:
        copy.wait_recv()
    rates = rate_blocks_ref[...]
    decay = lambda rates, steps: jnp.exp(-rates * (float(length) * steps))
    as_float = lambda value: lax.convert_element_type(value, jnp.float32)
    row_start = jnp.zeros(rates.shape, jnp.float32)
    row_total = decay(rates, as_float(ROW - 1 - y)) * state_ref[...]
    for k in range(1, ROW):
        state = row_states_ref[k - 1]
        row_start = row_start + jnp.where(k <= y, decay(rates, k - 1.0) * state, 0.0)
        row_total = row_total + decay(rates, as_float(ROW - 1 - wrapped(y - k, ROW))) * state
    total_ref[...] = row_total
    column_copies = [
        remote(total_ref.at[y], totals_ref.at[k - 1], column_sems.at[k - 1], at_column(k))
        for k in range(1, column)
    ]
    for copy in column_copies:
        copy.start()

    lax.fori_loop(groups // 2, groups, query_step, 0)

    for copy in column_copies:
        copy.wait_recv()
    quarter = rate_blocks_ref[y]
    start = jnp.zeros(quarter.shape, jnp.float32)
    for k in range(1, column):
        start = start + jnp.where(k <= z, decay(quarter, float(ROW * (k - 1))) * totals_ref[k - 1], 0.0)
    start_ref[y] = start
    start_copies = [
        remote(start_ref.at[y], start_ref.at[y], start_sems.at[k - 1], at_row(k)) for k in range(1, ROW)
    ]
    for copy in start_copies:
        copy.start()
    for copy in start_copies:
        copy.wait_recv()

    steps = as_float(y)
    for b in range(blocks):
        rows = slice(b * LANES, (b + 1) * LANES)
        incoming = decay(rates[b], steps) * start_ref[b] + row_start[b]
        across = jnp.transpose(incoming)
        same = iota((LANES, LANES), 1) // ORDER == iota((LANES, LANES), 0) // GROUP
        spread = jnp.where(same, jnp.concatenate([across] * (LANES // ORDER), axis=1), 0.0)
        carried = dot_split(split(spread), split(readout_ref[rows, :]), NN)
        gated_ref[rows, :] = (query_ref[rows, :] * (base_ref[rows, :] + carried)).astype(jnp.bfloat16)

    gated = gated_ref[...]
    part = out_ref.shape[0]
    half = part // 2

    def share(k, whose):
        owner = wrapped(x + k, RING) * 2 + whose
        rows = pl.ds(pl.multiple_of(owner * part, part), part)
        return jnp.dot(out_weight_ref[rows, :], gated, preferred_element_type=jnp.float32)

    pair_copies = [remote(given_ref.at[k], pair_ref.at[k], pair_sems.at[k], partner) for k in range(RING)]
    order = (2, 1, 3, 0)
    for k in order:
        given_ref[k] = share(k, 1 - core)
        pair_copies[k].start()
    for k in order:
        mine_ref[k] = share(k, core)

    top, bottom = pl.ds(0, half), pl.ds(half, half)
    relay_up = remote(mine_ref.at[2, top], relay_ref.at[0], ring_sems.at[0], at_ring(1))
    relay_down = remote(mine_ref.at[2, bottom], relay_ref.at[1], ring_sems.at[1], at_ring(-1))
    early_up = remote(mine_ref.at[1, bottom], last_ref.at[0, bottom], ring_sems.at[2], at_ring(1))
    early_down = remote(mine_ref.at[3, top], last_ref.at[1, top], ring_sems.at[3], at_ring(-1))
    late_up = remote(mine_ref.at[1, top], last_ref.at[0, top], ring_sems.at[4], at_ring(1))
    late_down = remote(mine_ref.at[3, bottom], last_ref.at[1, bottom], ring_sems.at[5], at_ring(-1))

    pair_copies[2].wait_recv()
    mine_ref[2] = mine_ref[2] + pair_ref[2]
    relay_up.start()
    relay_down.start()
    pair_copies[1].wait_recv()
    mine_ref[1] = mine_ref[1] + pair_ref[1]
    early_up.start()
    pair_copies[3].wait_recv()
    mine_ref[3] = mine_ref[3] + pair_ref[3]
    early_down.start()
    pair_copies[0].wait_recv()
    mine_ref[0] = mine_ref[0] + pair_ref[0]
    relay_up.wait_recv()
    mine_ref[1, top] = mine_ref[1, top] + relay_ref[0]
    late_up.start()
    relay_down.wait_recv()
    mine_ref[3, bottom] = mine_ref[3, bottom] + relay_ref[1]
    late_down.start()
    early_up.wait_recv()
    early_down.wait_recv()
    late_up.wait_recv()
    late_down.wait_recv()
    out_ref[...] = mine_ref[0] + last_ref[0] + last_ref[1]

    sent = halo_copies + [extra_copy] + row_copies + column_copies + start_copies + pair_copies
    sent += [relay_up, relay_down, early_up, early_down, late_up, late_down]
    for copy in sent:
        copy.wait_send()


def vmem():
    return pl.BlockSpec(memory_space=pltpu.VMEM)


def per_device(features, short_filter, medium_filter, rates, residues, skip_gain, out_weight):
    channels, length = features.shape[1:]
    groups = rates.shape[0]
    blocks = channels // LANES
    column = lax.axis_size("seq") // ROW
    part = out_weight.shape[0] // lax.axis_size("tp")
    f32 = jnp.float32
    weight = residues * jnp.sqrt(-jnp.expm1(-2.0 * rates))
    rate_blocks = jnp.repeat(rates.T, GROUP, axis=1).reshape(ORDER, blocks, LANES).transpose(1, 0, 2)
    tile = (ORDER, LANES)
    pairs = lambda n: pltpu.SemaphoreType.DMA((n, 2))
    return pl.pallas_call(
        layer_kernel,
        out_shape=jax.ShapeDtypeStruct((part, length), f32),
        in_specs=[vmem()] * 10,
        out_specs=vmem(),
        scratch_shapes=[
            pltpu.VMEM((3, channels, LANES), f32),
            pltpu.VMEM((3, 32, LANES), f32),
            pltpu.VMEM((3, 32, LANES), f32),
            pltpu.VMEM((3 * groups, length), f32),
            pltpu.VMEM((groups, length), f32),
            pltpu.VMEM((groups * ORDER, length), f32),
            pltpu.VMEM((groups * ORDER, length), f32),
            pltpu.VMEM((channels, length), f32),
            pltpu.VMEM((channels, length), f32),
            pltpu.VMEM((channels, length), f32),
            pltpu.VMEM((channels, length), jnp.bfloat16),
            pltpu.VMEM((blocks,) + tile, f32),
            pltpu.VMEM((ROW - 1, blocks) + tile, f32),
            pltpu.VMEM((blocks,) + tile, f32),
            pltpu.VMEM((column - 1,) + tile, f32),
            pltpu.VMEM((ROW,) + tile, f32),
            pltpu.VMEM((RING, part, length), f32),
            pltpu.VMEM((RING, part, length), f32),
            pltpu.VMEM((RING, part, length), f32),
            pltpu.VMEM((2, part // 2, length), f32),
            pltpu.VMEM((2, part, length), f32),
            pairs(4), pairs(ROW - 1), pairs(column - 1), pairs(ROW - 1), pairs(RING), pairs(6),
        ],
        compiler_params=pltpu.CompilerParams(
            collective_id=0, has_side_effects=True, vmem_limit_bytes=48 * 1024 * 1024
        ),
    )(
        features, short_filter.reshape(3 * groups, SHORT), medium_filter.reshape(3 * groups, MEDIUM),
        rates, weight, rates.reshape(-1, 1), weight.reshape(-1, 1), rate_blocks, skip_gain[:, None],
        out_weight,
    )


def solution(mesh):
    in_specs = (
        P(None, "tp", "seq"),
        P(None, "tp", None),
        P(None, "tp", None),
        P("tp", None),
        P("tp", None),
        P("tp"),
        P(None, "tp"),
    )
    out_specs = P("tp", "seq")
    return jax.shard_map(
        per_device, mesh=mesh, in_specs=in_specs, out_specs=out_specs, check_vma=False
    )
```

time: 255 us -> 89.6 us (0.35)
  waiting for transfers between devices: 197 us -> 0 us
  Pallas kernels: 23.6 us -> 81.4 us
  between operations: 13.6 us -> 0.08 us
  starting transfers between devices: 7.29 us -> 0 us
  local copies, waits for them, and re-layouts: 10.8 us -> 7.66 us
    all_gather x1 -> x0, waiting for transfers between devices: 141 us -> none  [per_device(): gathered = lax.all_gather(state, 'seq')]
    pallas_call x2 -> x1, Pallas kernels: 23.6 us -> 81.4 us  [per_device(): pl.pallas_call(layer_kernel, out_shape=jax.ShapeDtypeStruct((part, length...]
    reduce_scatter x1 -> x0, waiting for transfers between devices: 45.8 us -> none  [per_device(): return lax.psum_scatter(partial, 'tp', scatter_dimension=0, tiled=True)]
    ppermute x2 -> x0, waiting for transfers between devices: 9.79 us -> none  [passed_along(): return lax.ppermute(block, axis, [(i, i + 1) for i in range(devices - 1)])]
    ppermute x2 -> x0, starting transfers between devices: 7.21 us -> none  [passed_along(): return lax.ppermute(block, axis, [(i, i + 1) for i in range(devices - 1)])]
    unnamed x30 -> x10, local copies, waits for them, and re-layouts: 5 us -> 5.55 us
  transfers between devices with their start and end apart: 4 -> 0, of which waited for: 3 -> 0; matrix products, arithmetic and copies ran while one was open for 2% -> 0% of each run, Pallas kernels for 0% -> 0%
where the time goes in v2:
time: 89.6 us; the launch traced here: 89.2 us
  Pallas kernels  81.4 us (91%)
  local copies, waits for them, and re-layouts  7.66 us (9%)
    pallas_call x1, Pallas kernels, per_device(): pl.pallas_call(layer_kernel, out_shape=jax.ShapeDtypeStruct((part, length...  81.4 us
    unnamed x10, local copies, waits for them, and re-layouts  5.55 us

profile of v2, /device:TPU:1, one launch (start us, length us, event | category | flops | bytes accessed | tf_op | source)
XLA Modules:
  0.0 89.2 jit_solution(11272706852712108929)
XLA Ops:
  0.0 0.0 copy-start.1
  0.0 0.9 copy.28.rates_ref
  0.9 0.8 copy.25
  1.7 0.8 copy.22
  2.5 0.2 reshape.17.weight_rows_ref
  2.7 0.2 reshape.16.rate_rows_ref
  2.8 0.8 copy.31.gain_ref
  3.7 0.8 broadcast_in_dim.6
  4.5 0.1 reshape_reshape.3
  4.6 0.0 copy-done.1
  4.7 0.0 copy-start
  4.7 1.6 %copy-done = bf16[2048,512]{1,0:T(8,128)(2,1)S(1)} copy-done((bf16[2048,512]{1,0:T(8,128)(2,1)S(1)}, bf16[2048,512]{1,0:T(8,128)(2,1)}, u32[]{:S(2)}) %copy-start) | copy-done | bytes 2097176
  6.2 0.0 copy-start.2
  6.2 0.8 copy-done.2
  7.0 81.4 %shard_map.73 = f32[256,256]{1,0:T(8,128)S(1)} custom-call(f32[3,512,256]{2,1,0:T(8,128)S(1)} %copy-done.1, f32[96,7]{1,0:T(8,128)S(1)} %bitcast.7, f32[96,128]{1,0:T(8,128)S(1)} %bitcast.9, f32[32,16]{1,0:T(8,128)S(1)} %copy.28.rates_ref, f32[32,16]{1,0:T(8,128)S(1)} %sqrt_multiply_fusion.weight_ref, f32[512,1]{1,0:T(8,128)S(1)} %reshape.16.rate_rows_ref, ...), custom_call_target="tpu_custom_call" | custom-call | tf_op jit(solution)/shard_map/pallas_call | solution.py:308
  88.5 0.7 copy.35
  (2 shorter events, 0.0 us)
Async XLA Ops:
  0.0 4.6 %copy-start.1 = (f32[3,512,256]{2,1,0:T(8,128)S(1)}, f32[3,512,256]{2,1,0:T(8,128)}, u32[]{:S(2)}) copy-start(f32[3,512,256]{2,1,0:T(8,128)} %features_ref.1) | copy-start | bytes 4718596
  4.7 1.6 %copy-start = (bf16[2048,512]{1,0:T(8,128)(2,1)S(1)}, bf16[2048,512]{1,0:T(8,128)(2,1)}, u32[]{:S(2)}) copy-start(bf16[2048,512]{1,0:T(8,128)(2,1)} %out_weight_ref.1) | copy-start | bytes 6291460
  6.2 0.8 copy-start.2

commit v3 on v2

--- a/solution.py
+++ b/solution.py
@@ -14,6 +14,7 @@
 LANES = 128
 ROW = 4
 RING = 4
+SUB = 8
 
 
 def split(x):
@@ -38,45 +39,62 @@
     return lax.broadcasted_iota(jnp.int32, shape, axis)
 
 
+def upright(flat):
+    rows, columns = flat.shape
+    padded = jnp.concatenate([flat, jnp.zeros((rows, LANES - columns), jnp.float32)], axis=1)
+    padded = jnp.concatenate([padded, jnp.zeros((LANES - rows, LANES), jnp.float32)], axis=0)
+    return jnp.transpose(padded)[:columns]
+
+
 def filter_tables(short_ref, medium_ref, taps_ref):
-    medium = medium_ref[...]
-    wide = jnp.concatenate([medium, jnp.zeros_like(medium)], axis=1)
-    short = short_ref[...]
-    total = short[:, 0:1] * wide
-    for j in range(1, SHORT):
-        total = total + short[:, j : j + 1] * pltpu.roll(wide, j, 1)
-    taps_ref[...] = total
-
-
-def modal_tables(rates_ref, weight_ref, rate_rows_ref, weight_rows_ref, kernel_ref, ending_ref, readout_ref):
-    length = kernel_ref.shape[1]
+    branches, groups = medium_ref.shape[:2]
+    for i in range(branches):
+        medium, short = medium_ref[i], upright(short_ref[i])
+        wide = jnp.concatenate([medium, jnp.zeros_like(medium)], axis=1)
+        total = short[:, 0:1] * wide
+        for j in range(1, SHORT):
+            total = total + short[:, j : j + 1] * pltpu.roll(wide, j, 1)
+        taps_ref[i * groups : (i + 1) * groups, :] = total
+
+
+def modal_tables(rates_ref, weight_ref, rate_blocks_ref, kernel_ref, ending_ref, readout_ref):
+    groups, length = kernel_ref.shape
     steps = iota((1, length), 1).astype(jnp.float32)
-    rates, weight = rates_ref[...], weight_ref[...]
-    total = weight[:, 0:1] * jnp.exp(-rates[:, 0:1] * steps)
-    for n in range(1, ORDER):
-        total = total + weight[:, n : n + 1] * jnp.exp(-rates[:, n : n + 1] * steps)
-    kernel_ref[...] = total
-    rate_rows = rate_rows_ref[...]
-    ending_ref[...] = jnp.exp(-rate_rows * (length - 1.0 - steps))
-    readout_ref[...] = weight_rows_ref[...] * jnp.exp(-rate_rows * (steps + 1.0))
+    all_rates, all_weight = upright(rates_ref[...]), upright(weight_ref[...])
+    for b in range(groups // SUB):
+        rates = all_rates[b * SUB : (b + 1) * SUB]
+        weight = all_weight[b * SUB : (b + 1) * SUB]
+        total = jnp.zeros((SUB, length), jnp.float32)
+        for n in range(ORDER):
+            rate, share = rates[:, n : n + 1], weight[:, n : n + 1]
+            rows = slice((b * ORDER + n) * SUB, (b * ORDER + n + 1) * SUB)
+            total = total + share * jnp.exp(-rate * steps)
+            ending_ref[rows, :] = jnp.exp(-rate * (length - 1.0 - steps))
+            readout_ref[rows, :] = share * jnp.exp(-rate * (steps + 1.0))
+        kernel_ref[b * SUB : (b + 1) * SUB, :] = total
+        wide = jnp.broadcast_to(rates[:, None, :], (SUB, GROUP, LANES)).reshape(SUB * GROUP, LANES)
+        rate_blocks_ref[b] = jnp.transpose(wide)[:ORDER]
 
 
 def toeplitz(row, rows):
     return pltpu.roll(jnp.broadcast_to(row, (rows, row.shape[1])), 0, 1, stride=1, stride_axis=0)
 
 
-def filter_group(extra, halo, own, taps_row):
+def filter_matrix(taps_row):
     rolled = toeplitz(taps_row, LANES)
     near, middle = rolled[:, :LANES], rolled[:, LANES:]
     causal = iota((LANES, LANES), 1) >= iota((LANES, LANES), 0)
-    matrix = jnp.concatenate(
+    return split(jnp.concatenate(
         [jnp.where(causal, 0.0, near), middle, jnp.where(causal, near, 0.0)], axis=0
-    )
+    ))
+
+
+def filter_group(extra, halo, own, matrix):
     tiles = [extra, halo, own[:, :LANES], own[:, LANES:]]
     windows = jnp.concatenate(
         [jnp.concatenate(tiles[0:3], axis=1), jnp.concatenate(tiles[1:4], axis=1)], axis=0
     )
-    result = dot_split(split(windows), split(matrix), NN)
+    result = dot_split(split(windows), matrix, NN)
     return jnp.concatenate([result[:GROUP], result[GROUP:]], axis=1)
 
 
@@ -85,13 +103,15 @@
 
 
 def layer_kernel(
-    features_ref, short_ref, medium_ref, rates_ref, weight_ref, rate_rows_ref, weight_rows_ref,
-    rate_blocks_ref, gain_ref, out_weight_ref,
+    features_hbm, short_ref, medium_ref, rates_ref, weight_ref, gain_ref, out_weight_hbm,
     out_ref,
+    features_ref, out_weight_ref, rate_blocks_ref,
+    matrix_high_ref, matrix_low_ref, long_high_ref, long_low_ref,
     halo_ref, packed_ref, extra_ref, taps_ref, kernel_ref, ending_ref, readout_ref,
     product_ref, query_ref, base_ref, gated_ref,
     state_ref, row_states_ref, total_ref, totals_ref, start_ref,
     given_ref, mine_ref, pair_ref, relay_ref, last_ref,
+    near_sems, local_sems,
     halo_sems, row_sems, column_sems, start_sems, pair_sems, ring_sems,
 ):
     groups, length = kernel_ref.shape
@@ -108,6 +128,9 @@
     following, before = (wrapped(seq + 1, count), tp), (wrapped(seq - 1, count), tp)
     partner = (seq, x * 2 + 1 - core)
 
+    def signal(semaphore, device):
+        pl.semaphore_signal(semaphore, inc=1, device_id=device, device_id_type=pl.DeviceIdType.MESH)
+
     def remote(source, target, sems, device):
         return pltpu.make_async_remote_copy(
             src_ref=source, dst_ref=target, send_sem=sems.at[0], recv_sem=sems.at[1],
@@ -116,78 +139,120 @@
 
     barrier = pltpu.get_barrier_semaphore()
     peers = [following, before, partner, at_ring(1), at_ring(-1)]
-    peers += [at_row(k) for k in range(1, ROW)] + [at_column(k) for k in range(1, column)]
+    peers += [at_row(1), at_row(-1), at_column(1), at_column(-1)]
     for peer in peers:
-        pl.semaphore_signal(barrier, inc=1, device_id=peer, device_id_type=pl.DeviceIdType.MESH)
+        signal(barrier, peer)
+    loads = [pltpu.make_async_copy(features_hbm.at[i], features_ref.at[i], local_sems.at[i]) for i in range(3)]
+    loads.append(pltpu.make_async_copy(out_weight_hbm, out_weight_ref, local_sems.at[3]))
+    for i in (1, 2, 0, 3):
+        loads[i].start()
+    halo_copies = [
+        [
+            remote(
+                features_hbm.at[i, pl.ds(b * LANES, LANES), pl.ds(length - LANES, LANES)],
+                halo_ref.at[i, pl.ds(b * LANES, LANES)], halo_sems.at[i * blocks + b], following,
+            )
+            for b in range(blocks)
+        ]
+        for i in range(3)
+    ]
+    extra_copy = remote(packed_ref, extra_ref, halo_sems.at[3 * blocks], following)
     lane = iota((32, LANES), 1) // 8
-    for i in range(3):
+    for i in (1, 2, 0):
+        loads[i].wait()
         packed = jnp.zeros((32, LANES), jnp.float32)
         for p in range(channels // 32):
             moved = pltpu.roll(features_ref[i, 32 * p : 32 * p + 32, 0:LANES], (8 * p + 8) % LANES, 1)
             packed = jnp.where(lane == p, moved, packed)
         packed_ref[i] = packed
     pl.semaphore_wait(barrier, len(peers))
-
-    halo_copies = [
-        remote(features_ref.at[i, :, pl.ds(length - LANES, LANES)], halo_ref.at[i], halo_sems.at[i], following)
-        for i in range(3)
-    ]
-    extra_copy = remote(packed_ref, extra_ref, halo_sems.at[3], following)
     extra_copy.start()
-    for i in (1, 2, 0):
-        halo_copies[i].start()
-
+    for b in range(blocks):
+        halo_copies[1][b].start()
+        halo_copies[2][b].start()
+    for b in range(blocks):
+        halo_copies[0][b].start()
+
+    signal(near_sems.at[3], at_row(1))
+    signal(near_sems.at[3], at_row(-1))
+    signal(near_sems.at[0], at_column(1))
+    signal(near_sems.at[0], at_column(-1))
     filter_tables(short_ref, medium_ref, taps_ref)
-    modal_tables(rates_ref, weight_ref, rate_rows_ref, weight_rows_ref, kernel_ref, ending_ref, readout_ref)
+    pl.semaphore_wait(near_sems.at[3], 2)
+    pl.semaphore_wait(near_sems.at[0], 2)
+    signal(near_sems.at[1], at_column(2))
+    signal(near_sems.at[1], at_column(-2))
+    modal_tables(rates_ref, weight_ref, rate_blocks_ref, kernel_ref, ending_ref, readout_ref)
+    pl.semaphore_wait(near_sems.at[1], 2)
+    signal(near_sems.at[2], at_column(4))
+    signal(near_sems.at[2], at_column(-4))
     inner = seq > 0
 
-    def branch(i, g):
+    def matrices_step(g, carry):
+        for i in (1, 2):
+            place = (i - 1) * groups + g
+            high, low = filter_matrix(taps_ref[pl.ds(i * groups + g, 1), :])
+            matrix_high_ref[place] = high
+            matrix_low_ref[place] = low
+        rolled = toeplitz(kernel_ref[pl.ds(g, 1), :], length)
+        causal = iota((length, length), 1) >= iota((length, length), 0)
+        high, low = split(jnp.where(causal, rolled, 0.0))
+        long_high_ref[g] = high
+        long_low_ref[g] = low
+        return carry
+
+    def branch(i, g, matrix):
         rows = pl.ds(pl.multiple_of(g * GROUP, GROUP), GROUP)
         packed = extra_ref[i, pl.ds(pl.multiple_of(lax.rem(g, 2) * GROUP, GROUP), GROUP), :]
         extra = pltpu.roll(packed, LANES - 8 - 8 * (g // 2), 1)
         zero = jnp.zeros((GROUP, LANES), jnp.float32)
         return filter_group(
             jnp.where(inner, extra, zero), jnp.where(inner, halo_ref[i, rows, :], zero),
-            features_ref[i, rows, :], taps_ref[pl.ds(i * groups + g, 1), :],
+            features_ref[i, rows, :], matrix,
         )
 
-    def product_step(g, carry):
-        rows = pl.ds(pl.multiple_of(g * GROUP, GROUP), GROUP)
-        product = branch(1, g) * branch(2, g)
-        product_ref[rows, :] = product
-        rolled = toeplitz(kernel_ref[pl.ds(g, 1), :], length)
-        causal = iota((length, length), 1) >= iota((length, length), 0)
-        inside = dot_split(split(product), split(jnp.where(causal, rolled, 0.0)), NN)
-        base_ref[rows, :] = inside + gain_ref[rows, :] * product
+    def product_step(half, carry):
+        for g in [half * 4 + u for u in range(4)]:
+            rows = pl.ds(pl.multiple_of(g * GROUP, GROUP), GROUP)
+            key = branch(1, g, (matrix_high_ref[g], matrix_low_ref[g]))
+            value = branch(2, g, (matrix_high_ref[groups + g], matrix_low_ref[groups + g]))
+            product = key * value
+            product_ref[rows, :] = product
+            base_ref[rows, :] = dot_split(split(product), (long_high_ref[g], long_low_ref[g]), NN)
         return carry
 
-    def query_step(g, carry):
-        rows = pl.ds(pl.multiple_of(g * GROUP, GROUP), GROUP)
-        query_ref[rows, :] = branch(0, g)
+    def query_step(half, carry):
+        for g in [half * 2 + u for u in range(2)]:
+            rows = pl.ds(pl.multiple_of(g * GROUP, GROUP), GROUP)
+            query_ref[rows, :] = branch(0, g, filter_matrix(taps_ref[pl.ds(g, 1), :]))
         return carry
 
+    lax.fori_loop(0, groups, matrices_step, 0)
+    pl.semaphore_wait(near_sems.at[2], 2)
     extra_copy.wait_recv()
-    halo_copies[1].wait_recv()
-    halo_copies[2].wait_recv()
-    lax.fori_loop(0, groups, product_step, 0)
-
-    same = iota((LANES, LANES), 0) // ORDER == iota((LANES, LANES), 1) // GROUP
+    same = lax.rem(iota((LANES, LANES), 0), SUB) == iota((LANES, LANES), 1) // GROUP
+    quarter_steps = groups // blocks // 4
     for b in range(blocks):
+        halo_copies[1][b].wait_recv()
+        halo_copies[2][b].wait_recv()
+        lax.fori_loop(b * quarter_steps, (b + 1) * quarter_steps, product_step, 0)
         rows = slice(b * LANES, (b + 1) * LANES)
         full = dot_split(split(ending_ref[rows, :]), split(product_ref[rows, :]), NT)
         full = jnp.where(same, full, 0.0)
-        total = full[0:ORDER]
-        for k in range(1, LANES // ORDER):
-            total = total + full[k * ORDER : (k + 1) * ORDER]
-        state_ref[b] = total
+        state_ref[b] = jnp.sum(full.reshape(ORDER, SUB, LANES), axis=1)
     row_copies = [
         remote(state_ref, row_states_ref.at[k - 1], row_sems.at[k - 1], at_row(k)) for k in range(1, ROW)
     ]
     for copy in row_copies:
         copy.start()
-
-    halo_copies[0].wait_recv()
-    lax.fori_loop(0, groups // 2, query_step, 0)
+    for b in range(blocks):
+        rows = slice(b * LANES, (b + 1) * LANES)
+        gain = jnp.transpose(jnp.broadcast_to(gain_ref[b : b + 1, :], (LANES, LANES)))
+        base_ref[rows, :] = base_ref[rows, :] + jnp.concatenate([gain] * (length // LANES), axis=1) * product_ref[rows, :]
+
+    for copy in halo_copies[0]:
+        copy.wait_recv()
+    lax.fori_loop(0, groups // 4, query_step, 0)
 
     for copy in row_copies:
         copy.wait_recv()
@@ -208,7 +273,7 @@
     for copy in column_copies:
         copy.start()
 
-    lax.fori_loop(groups // 2, groups, query_step, 0)
+    lax.fori_loop(groups // 4, groups // 2, query_step, 0)
 
     for copy in column_copies:
         copy.wait_recv()
@@ -229,12 +294,12 @@
     for b in range(blocks):
         rows = slice(b * LANES, (b + 1) * LANES)
         incoming = decay(rates[b], steps) * start_ref[b] + row_start[b]
-        across = jnp.transpose(incoming)
-        same = iota((LANES, LANES), 1) // ORDER == iota((LANES, LANES), 0) // GROUP
-        spread = jnp.where(same, jnp.concatenate([across] * (LANES // ORDER), axis=1), 0.0)
+        tall = jnp.broadcast_to(incoming[:, None, :], (ORDER, SUB, LANES)).reshape(LANES, LANES)
+        spread = jnp.transpose(jnp.where(same, tall, 0.0))
         carried = dot_split(split(spread), split(readout_ref[rows, :]), NN)
         gated_ref[rows, :] = (query_ref[rows, :] * (base_ref[rows, :] + carried)).astype(jnp.bfloat16)
 
+    loads[3].wait()
     gated = gated_ref[...]
     part = out_ref.shape[0]
     half = part // 2
@@ -284,14 +349,10 @@
     late_down.wait_recv()
     out_ref[...] = mine_ref[0] + last_ref[0] + last_ref[1]
 
-    sent = halo_copies + [extra_copy] + row_copies + column_copies + start_copies + pair_copies
+    sent = halo_copies[0] + halo_copies[1] + halo_copies[2] + [extra_copy] + row_copies + column_copies + start_copies + pair_copies
     sent += [relay_up, relay_down, early_up, early_down, late_up, late_down]
     for copy in sent:
         copy.wait_send()
-
-
-def vmem():
-    return pl.BlockSpec(memory_space=pltpu.VMEM)
 
 
 def per_device(features, short_filter, medium_filter, rates, residues, skip_gain, out_weight):
@@ -302,15 +363,24 @@
     part = out_weight.shape[0] // lax.axis_size("tp")
     f32 = jnp.float32
     weight = residues * jnp.sqrt(-jnp.expm1(-2.0 * rates))
-    rate_blocks = jnp.repeat(rates.T, GROUP, axis=1).reshape(ORDER, blocks, LANES).transpose(1, 0, 2)
     tile = (ORDER, LANES)
+    half = jnp.bfloat16
+    vmem = pl.BlockSpec(memory_space=pltpu.VMEM)
+    hbm = pl.BlockSpec(memory_space=pltpu.HBM)
     pairs = lambda n: pltpu.SemaphoreType.DMA((n, 2))
     return pl.pallas_call(
         layer_kernel,
         out_shape=jax.ShapeDtypeStruct((part, length), f32),
-        in_specs=[vmem()] * 10,
-        out_specs=vmem(),
+        in_specs=[hbm] + [vmem] * 5 + [hbm],
+        out_specs=vmem,
         scratch_shapes=[
+            pltpu.VMEM(features.shape, f32),
+            pltpu.VMEM(out_weight.shape, half),
+            pltpu.VMEM((blocks,) + tile, f32),
+            pltpu.VMEM((2 * groups, 3 * LANES, LANES), half),
+            pltpu.VMEM((2 * groups, 3 * LANES, LANES), half),
+            pltpu.VMEM((groups, length, length), half),
+            pltpu.VMEM((groups, length, length), half),
             pltpu.VMEM((3, channels, LANES), f32),
             pltpu.VMEM((3, 32, LANES), f32),
             pltpu.VMEM((3, 32, LANES), f32),
@@ -321,7 +391,7 @@
             pltpu.VMEM((channels, length), f32),
             pltpu.VMEM((channels, length), f32),
             pltpu.VMEM((channels, length), f32),
-            pltpu.VMEM((channels, length), jnp.bfloat16),
+            pltpu.VMEM((channels, length), half),
             pltpu.VMEM((blocks,) + tile, f32),
             pltpu.VMEM((ROW - 1, blocks) + tile, f32),
             pltpu.VMEM((blocks,) + tile, f32),
@@ -332,15 +402,15 @@
             pltpu.VMEM((RING, part, length), f32),
             pltpu.VMEM((2, part // 2, length), f32),
             pltpu.VMEM((2, part, length), f32),
-            pairs(4), pairs(ROW - 1), pairs(column - 1), pairs(ROW - 1), pairs(RING), pairs(6),
+            pltpu.SemaphoreType.REGULAR((4,)),
+            pltpu.SemaphoreType.DMA((4,)),
+            pairs(3 * blocks + 1), pairs(ROW - 1), pairs(column - 1), pairs(ROW - 1), pairs(RING), pairs(6),
         ],
         compiler_params=pltpu.CompilerParams(
-            collective_id=0, has_side_effects=True, vmem_limit_bytes=48 * 1024 * 1024
+            collective_id=0, has_side_effects=True, vmem_limit_bytes=58 * 1024 * 1024
         ),
     )(
-        features, short_filter.reshape(3 * groups, SHORT), medium_filter.reshape(3 * groups, MEDIUM),
-        rates, weight, rates.reshape(-1, 1), weight.reshape(-1, 1), rate_blocks, skip_gain[:, None],
-        out_weight,
+        features, jnp.swapaxes(short_filter, 1, 2), medium_filter, rates.T, weight.T, skip_gain.reshape(blocks, LANES), out_weight,
     )
 
 

time: 89.6 us -> 70.7 us (0.79)
  Pallas kernels: 81.4 us -> 67.5 us
  local copies, waits for them, and re-layouts: 7.66 us -> 1.67 us
  other arithmetic: 0.02 us -> 1.33 us
    pallas_call x1, Pallas kernels: 81.4 us -> 67.5 us  [per_device(): pl.pallas_call(layer_kernel, out_shape=jax.ShapeDtypeStruct((part, length...]
    unnamed x10 -> x1, local copies, waits for them, and re-layouts: 5.55 us -> 1.67 us
    broadcast_in_dim x2 -> x0, local copies, waits for them, and re-layouts: 1.64 us -> none  [the longest x1 0.82 us: per_device(): jnp.repeat(rates.T, GROUP, axis=1).reshape(ORDER, blocks, LANES)]
    transpose x0 -> x1, other arithmetic: none -> 1.33 us  [per_device(): return pl.pallas_call(layer_kernel, out_shape=jax.ShapeDtypeStruct((part,...]
where the time goes in v3:
time: 70.7 us; the launch traced here: 70.5 us
  Pallas kernels  67.5 us (95%)
  local copies, waits for them, and re-layouts  1.67 us (2%)
  other arithmetic  1.33 us (2%)
    pallas_call x1, Pallas kernels, per_device(): pl.pallas_call(layer_kernel, out_shape=jax.ShapeDtypeStruct((part, length...  67.5 us
    unnamed x1, local copies, waits for them, and re-layouts  1.67 us

profile of v3, /device:TPU:1, one launch (start us, length us, event | category | flops | bytes accessed | tf_op | source)
XLA Modules:
  0.0 70.5 jit_solution(3855132461967459349)
XLA Ops:
  0.0 1.3 %multiply_bitcast_fusion.weight_ref = f32[16,32]{1,0:T(8,128)} fusion(f32[32,16]{0,1:T(8,128)} %param.11, f32[32,16]{0,1:T(8,128)} %param.10), kind=kLoop, calls=%fused_computation | loop fusion | flops 1536 | bytes 6144 | tf_op jit(solution)/shard_map/transpose | solution.py:413
  1.3 67.5 %shard_map.73 = f32[256,256]{1,0:T(8,128)} custom-call(f32[3,512,256]{2,1,0:T(8,128)} %features_hbm.1, f32[3,7,32]{2,1,0:T(8,128)} %bitcast.6, f32[3,32,128]{2,1,0:T(8,128)} %medium_ref.1, f32[16,32]{1,0:T(8,128)} %bitcast.5, f32[16,32]{1,0:T(8,128)} %multiply_bitcast_fusion.weight_ref, f32[4,128]{1,0:T(4,128)} %bitcast.7, bf16[2048,512]{1,0:T(8,128)(2,1)} %out_weight_hbm.1), custom_call_target="tpu_custom_call" | custom-call | tf_op jit(solution)/shard_map/pallas_call | solution.py:371
  68.8 1.7 %copy.9 = f32[256,256]{1,0:T(8,128)} copy(f32[256,256]{1,0:T(8,128)} %shard_map.73) | data formatting | bytes 524288

commit v4 on v3

--- a/solution.py
+++ b/solution.py
@@ -57,10 +57,19 @@
         taps_ref[i * groups : (i + 1) * groups, :] = total
 
 
-def modal_tables(rates_ref, weight_ref, rate_blocks_ref, kernel_ref, ending_ref, readout_ref):
+def one_less_decay(power):
+    total = jnp.ones_like(power)
+    for order in range(8, 1, -1):
+        total = 1.0 - power * (1.0 / order) * total
+    return power * total
+
+
+def modal_tables(rates_ref, residues_ref, rate_blocks_ref, kernel_ref, ending_ref, readout_ref):
     groups, length = kernel_ref.shape
     steps = iota((1, length), 1).astype(jnp.float32)
-    all_rates, all_weight = upright(rates_ref[...]), upright(weight_ref[...])
+    flat_rates = rates_ref[...]
+    flat_weight = residues_ref[...] * jnp.sqrt(one_less_decay(2.0 * flat_rates))
+    all_rates, all_weight = upright(flat_rates), upright(flat_weight)
     for b in range(groups // SUB):
         rates = all_rates[b * SUB : (b + 1) * SUB]
         weight = all_weight[b * SUB : (b + 1) * SUB]
@@ -89,6 +98,22 @@
     ))
 
 
+def long_matrix(row):
+    rolled = toeplitz(row, LANES)
+    near, middle = rolled[:, :LANES], rolled[:, LANES:]
+    causal = iota((LANES, LANES), 1) >= iota((LANES, LANES), 0)
+    return split(jnp.concatenate([middle, jnp.where(causal, near, 0.0)], axis=0))
+
+
+def long_group(product, matrix):
+    first, second = product[:, :LANES], product[:, LANES:]
+    windows = jnp.concatenate(
+        [jnp.concatenate([jnp.zeros_like(first), first], axis=1), product], axis=0
+    )
+    result = dot_split(split(windows), matrix, NN)
+    return jnp.concatenate([result[:GROUP], result[GROUP:]], axis=1)
+
+
 def filter_group(extra, halo, own, matrix):
     tiles = [extra, halo, own[:, :LANES], own[:, LANES:]]
     windows = jnp.concatenate(
@@ -103,9 +128,9 @@
 
 
 def layer_kernel(
-    features_hbm, short_ref, medium_ref, rates_ref, weight_ref, gain_ref, out_weight_hbm,
+    features_hbm, short_hbm, medium_hbm, rates_hbm, residues_hbm, gain_hbm, out_weight_hbm,
     out_ref,
-    features_ref, out_weight_ref, rate_blocks_ref,
+    features_ref, short_ref, medium_ref, rates_ref, residues_ref, gain_ref, out_weight_ref, rate_blocks_ref,
     matrix_high_ref, matrix_low_ref, long_high_ref, long_low_ref,
     halo_ref, packed_ref, extra_ref, taps_ref, kernel_ref, ending_ref, readout_ref,
     product_ref, query_ref, base_ref, gated_ref,
@@ -142,9 +167,11 @@
     peers += [at_row(1), at_row(-1), at_column(1), at_column(-1)]
     for peer in peers:
         signal(barrier, peer)
+    whole = [short_hbm, medium_hbm, rates_hbm, residues_hbm, gain_hbm, out_weight_hbm]
+    kept = [short_ref, medium_ref, rates_ref, residues_ref, gain_ref, out_weight_ref]
     loads = [pltpu.make_async_copy(features_hbm.at[i], features_ref.at[i], local_sems.at[i]) for i in range(3)]
-    loads.append(pltpu.make_async_copy(out_weight_hbm, out_weight_ref, local_sems.at[3]))
-    for i in (1, 2, 0, 3):
+    loads += [pltpu.make_async_copy(a, b, local_sems.at[3 + k]) for k, (a, b) in enumerate(zip(whole, kept))]
+    for i in (1, 2, 0, 3, 4, 5, 6, 7, 8):
         loads[i].start()
     halo_copies = [
         [
@@ -158,6 +185,9 @@
     ]
     extra_copy = remote(packed_ref, extra_ref, halo_sems.at[3 * blocks], following)
     lane = iota((32, LANES), 1) // 8
+    pl.semaphore_wait(barrier, len(peers))
+    halo_copies[1][0].start()
+    halo_copies[2][0].start()
     for i in (1, 2, 0):
         loads[i].wait()
         packed = jnp.zeros((32, LANES), jnp.float32)
@@ -165,9 +195,8 @@
             moved = pltpu.roll(features_ref[i, 32 * p : 32 * p + 32, 0:LANES], (8 * p + 8) % LANES, 1)
             packed = jnp.where(lane == p, moved, packed)
         packed_ref[i] = packed
-    pl.semaphore_wait(barrier, len(peers))
     extra_copy.start()
-    for b in range(blocks):
+    for b in range(1, blocks):
         halo_copies[1][b].start()
         halo_copies[2][b].start()
     for b in range(blocks):
@@ -177,28 +206,29 @@
     signal(near_sems.at[3], at_row(-1))
     signal(near_sems.at[0], at_column(1))
     signal(near_sems.at[0], at_column(-1))
+    for i in range(3, 8):
+        loads[i].wait()
     filter_tables(short_ref, medium_ref, taps_ref)
     pl.semaphore_wait(near_sems.at[3], 2)
     pl.semaphore_wait(near_sems.at[0], 2)
     signal(near_sems.at[1], at_column(2))
     signal(near_sems.at[1], at_column(-2))
-    modal_tables(rates_ref, weight_ref, rate_blocks_ref, kernel_ref, ending_ref, readout_ref)
+    modal_tables(rates_ref, residues_ref, rate_blocks_ref, kernel_ref, ending_ref, readout_ref)
     pl.semaphore_wait(near_sems.at[1], 2)
     signal(near_sems.at[2], at_column(4))
     signal(near_sems.at[2], at_column(-4))
     inner = seq > 0
 
-    def matrices_step(g, carry):
-        for i in (1, 2):
-            place = (i - 1) * groups + g
-            high, low = filter_matrix(taps_ref[pl.ds(i * groups + g, 1), :])
-            matrix_high_ref[place] = high
-            matrix_low_ref[place] = low
-        rolled = toeplitz(kernel_ref[pl.ds(g, 1), :], length)
-        causal = iota((length, length), 1) >= iota((length, length), 0)
-        high, low = split(jnp.where(causal, rolled, 0.0))
-        long_high_ref[g] = high
-        long_low_ref[g] = low
+    def matrices_step(half, carry):
+        for g in [half * 2 + u for u in range(2)]:
+            for i in (1, 2):
+                place = (i - 1) * groups + g
+                high, low = filter_matrix(taps_ref[pl.ds(i * groups + g, 1), :])
+                matrix_high_ref[place] = high
+                matrix_low_ref[place] = low
+            high, low = long_matrix(kernel_ref[pl.ds(g, 1), :])
+            long_high_ref[g] = high
+            long_low_ref[g] = low
         return carry
 
     def branch(i, g, matrix):
@@ -218,7 +248,7 @@
             value = branch(2, g, (matrix_high_ref[groups + g], matrix_low_ref[groups + g]))
             product = key * value
             product_ref[rows, :] = product
-            base_ref[rows, :] = dot_split(split(product), (long_high_ref[g], long_low_ref[g]), NN)
+            base_ref[rows, :] = long_group(product, (long_high_ref[g], long_low_ref[g]))
         return carry
 
     def query_step(half, carry):
@@ -227,7 +257,7 @@
             query_ref[rows, :] = branch(0, g, filter_matrix(taps_ref[pl.ds(g, 1), :]))
         return carry
 
-    lax.fori_loop(0, groups, matrices_step, 0)
+    lax.fori_loop(0, groups // 2, matrices_step, 0)
     pl.semaphore_wait(near_sems.at[2], 2)
     extra_copy.wait_recv()
     same = lax.rem(iota((LANES, LANES), 0), SUB) == iota((LANES, LANES), 1) // GROUP
@@ -250,21 +280,18 @@
         gain = jnp.transpose(jnp.broadcast_to(gain_ref[b : b + 1, :], (LANES, LANES)))
         base_ref[rows, :] = base_ref[rows, :] + jnp.concatenate([gain] * (length // LANES), axis=1) * product_ref[rows, :]
 
-    for copy in halo_copies[0]:
-        copy.wait_recv()
-    lax.fori_loop(0, groups // 4, query_step, 0)
-
-    for copy in row_copies:
-        copy.wait_recv()
     rates = rate_blocks_ref[...]
     decay = lambda rates, steps: jnp.exp(-rates * (float(length) * steps))
     as_float = lambda value: lax.convert_element_type(value, jnp.float32)
+    to_total = [decay(rates, as_float(ROW - 1 - wrapped(y - k, ROW))) for k in range(ROW)]
+    to_start = [jnp.where(k <= y, decay(rates, k - 1.0), 0.0) for k in range(1, ROW)]
     row_start = jnp.zeros(rates.shape, jnp.float32)
-    row_total = decay(rates, as_float(ROW - 1 - y)) * state_ref[...]
+    row_total = to_total[0] * state_ref[...]
     for k in range(1, ROW):
+        row_copies[k - 1].wait_recv()
         state = row_states_ref[k - 1]
-        row_start = row_start + jnp.where(k <= y, decay(rates, k - 1.0) * state, 0.0)
-        row_total = row_total + decay(rates, as_float(ROW - 1 - wrapped(y - k, ROW))) * state
+        row_start = row_start + to_start[k - 1] * state
+        row_total = row_total + to_total[k] * state
     total_ref[...] = row_total
     column_copies = [
         remote(total_ref.at[y], totals_ref.at[k - 1], column_sems.at[k - 1], at_column(k))
@@ -273,14 +300,19 @@
     for copy in column_copies:
         copy.start()
 
-    lax.fori_loop(groups // 4, groups // 2, query_step, 0)
-
-    for copy in column_copies:
+    for copy in halo_copies[0]:
         copy.wait_recv()
+    lax.fori_loop(0, groups // 2, query_step, 0)
+
     quarter = rate_blocks_ref[y]
+    to_here = [
+        jnp.where(k <= z, decay(quarter, float(ROW * (k - 1))), 0.0) for k in range(1, column)
+    ]
+    through_row = decay(rates, as_float(y))
     start = jnp.zeros(quarter.shape, jnp.float32)
     for k in range(1, column):
-        start = start + jnp.where(k <= z, decay(quarter, float(ROW * (k - 1))) * totals_ref[k - 1], 0.0)
+        column_copies[k - 1].wait_recv()
+        start = start + to_here[k - 1] * totals_ref[k - 1]
     start_ref[y] = start
     start_copies = [
         remote(start_ref.at[y], start_ref.at[y], start_sems.at[k - 1], at_row(k)) for k in range(1, ROW)
@@ -290,16 +322,15 @@
     for copy in start_copies:
         copy.wait_recv()
 
-    steps = as_float(y)
     for b in range(blocks):
         rows = slice(b * LANES, (b + 1) * LANES)
-        incoming = decay(rates[b], steps) * start_ref[b] + row_start[b]
+        incoming = through_row[b] * start_ref[b] + row_start[b]
         tall = jnp.broadcast_to(incoming[:, None, :], (ORDER, SUB, LANES)).reshape(LANES, LANES)
         spread = jnp.transpose(jnp.where(same, tall, 0.0))
         carried = dot_split(split(spread), split(readout_ref[rows, :]), NN)
         gated_ref[rows, :] = (query_ref[rows, :] * (base_ref[rows, :] + carried)).astype(jnp.bfloat16)
 
-    loads[3].wait()
+    loads[8].wait()
     gated = gated_ref[...]
     part = out_ref.shape[0]
     half = part // 2
@@ -310,13 +341,6 @@
         return jnp.dot(out_weight_ref[rows, :], gated, preferred_element_type=jnp.float32)
 
     pair_copies = [remote(given_ref.at[k], pair_ref.at[k], pair_sems.at[k], partner) for k in range(RING)]
-    order = (2, 1, 3, 0)
-    for k in order:
-        given_ref[k] = share(k, 1 - core)
-        pair_copies[k].start()
-    for k in order:
-        mine_ref[k] = share(k, core)
-
     top, bottom = pl.ds(0, half), pl.ds(half, half)
     relay_up = remote(mine_ref.at[2, top], relay_ref.at[0], ring_sems.at[0], at_ring(1))
     relay_down = remote(mine_ref.at[2, bottom], relay_ref.at[1], ring_sems.at[1], at_ring(-1))
@@ -325,18 +349,30 @@
     late_up = remote(mine_ref.at[1, top], last_ref.at[0, top], ring_sems.at[4], at_ring(1))
     late_down = remote(mine_ref.at[3, bottom], last_ref.at[1, bottom], ring_sems.at[5], at_ring(-1))
 
-    pair_copies[2].wait_recv()
-    mine_ref[2] = mine_ref[2] + pair_ref[2]
+    def offer(k):
+        given_ref[k] = share(k, 1 - core)
+        pair_copies[k].start()
+
+    def meet(k):
+        pair_copies[k].wait_recv()
+        mine_ref[k] = mine_ref[k] + pair_ref[k]
+
+    offer(2)
+    offer(1)
+    mine_ref[2] = share(2, core)
+    offer(3)
+    meet(2)
     relay_up.start()
     relay_down.start()
-    pair_copies[1].wait_recv()
-    mine_ref[1] = mine_ref[1] + pair_ref[1]
+    mine_ref[1] = share(1, core)
+    meet(1)
     early_up.start()
-    pair_copies[3].wait_recv()
-    mine_ref[3] = mine_ref[3] + pair_ref[3]
+    mine_ref[3] = share(3, core)
+    meet(3)
     early_down.start()
-    pair_copies[0].wait_recv()
-    mine_ref[0] = mine_ref[0] + pair_ref[0]
+    offer(0)
+    mine_ref[0] = share(0, core)
+    meet(0)
     relay_up.wait_recv()
     mine_ref[1, top] = mine_ref[1, top] + relay_ref[0]
     late_up.start()
@@ -362,7 +398,6 @@
     column = lax.axis_size("seq") // ROW
     part = out_weight.shape[0] // lax.axis_size("tp")
     f32 = jnp.float32
-    weight = residues * jnp.sqrt(-jnp.expm1(-2.0 * rates))
     tile = (ORDER, LANES)
     half = jnp.bfloat16
     vmem = pl.BlockSpec(memory_space=pltpu.VMEM)
@@ -370,17 +405,22 @@
     pairs = lambda n: pltpu.SemaphoreType.DMA((n, 2))
     return pl.pallas_call(
         layer_kernel,
-        out_shape=jax.ShapeDtypeStruct((part, length), f32),
-        in_specs=[hbm] + [vmem] * 5 + [hbm],
+        out_shape=pltpu.VMEM((part, length), f32),
+        in_specs=[hbm] * 7,
         out_specs=vmem,
         scratch_shapes=[
             pltpu.VMEM(features.shape, f32),
+            pltpu.VMEM((3, SHORT, groups), f32),
+            pltpu.VMEM(medium_filter.shape, f32),
+            pltpu.VMEM((ORDER, groups), f32),
+            pltpu.VMEM((ORDER, groups), f32),
+            pltpu.VMEM((blocks, LANES), f32),
             pltpu.VMEM(out_weight.shape, half),
             pltpu.VMEM((blocks,) + tile, f32),
             pltpu.VMEM((2 * groups, 3 * LANES, LANES), half),
             pltpu.VMEM((2 * groups, 3 * LANES, LANES), half),
-            pltpu.VMEM((groups, length, length), half),
-            pltpu.VMEM((groups, length, length), half),
+            pltpu.VMEM((groups, 2 * LANES, LANES), half),
+            pltpu.VMEM((groups, 2 * LANES, LANES), half),
             pltpu.VMEM((3, channels, LANES), f32),
             pltpu.VMEM((3, 32, LANES), f32),
             pltpu.VMEM((3, 32, LANES), f32),
@@ -403,14 +443,14 @@
             pltpu.VMEM((2, part // 2, length), f32),
             pltpu.VMEM((2, part, length), f32),
             pltpu.SemaphoreType.REGULAR((4,)),
-            pltpu.SemaphoreType.DMA((4,)),
+            pltpu.SemaphoreType.DMA((9,)),
             pairs(3 * blocks + 1), pairs(ROW - 1), pairs(column - 1), pairs(ROW - 1), pairs(RING), pairs(6),
         ],
         compiler_params=pltpu.CompilerParams(
             collective_id=0, has_side_effects=True, vmem_limit_bytes=58 * 1024 * 1024
         ),
     )(
-        features, jnp.swapaxes(short_filter, 1, 2), medium_filter, rates.T, weight.T, skip_gain.reshape(blocks, LANES), out_weight,
+        features, jnp.swapaxes(short_filter, 1, 2), medium_filter, rates.T, residues.T, skip_gain.reshape(blocks, LANES), out_weight,
     )
 
 

time: 70.7 us -> 65.1 us (0.921)
  Pallas kernels: 67.5 us -> 64.2 us
  other arithmetic: 1.33 us -> 0 us
  local copies, waits for them, and re-layouts: 1.67 us -> 0.71 us
    pallas_call x1, Pallas kernels: 67.5 us -> 64.2 us  [per_device(): pl.pallas_call(layer_kernel, out_shape=pltpu.VMEM((part, length), f32), i...]
    transpose x1 -> x0, other arithmetic: 1.33 us -> none  [per_device(): return pl.pallas_call(layer_kernel, out_shape=jax.ShapeDtypeStruct((part,...]
    unnamed x1, local copies, waits for them, and re-layouts: 1.67 us -> 0.71 us
where the time goes in v4:
time: 65.1 us; the launch traced here: 65 us
  Pallas kernels  64.2 us (99%)
  local copies, waits for them, and re-layouts  0.71 us (1%)
    pallas_call x1, Pallas kernels, per_device(): pl.pallas_call(layer_kernel, out_shape=pltpu.VMEM((part, length), f32), i...  64.2 us

profile of v4, /device:TPU:1, one launch (start us, length us, event | category | flops | bytes accessed | tf_op | source)
XLA Modules:
  0.0 65.0 jit_solution(13984706113542244325)
XLA Ops:
  0.0 64.2 %shard_map.73 = f32[256,256]{1,0:T(8,128)S(1)} custom-call(f32[3,512,256]{2,1,0:T(8,128)} %features_hbm.1, f32[3,7,32]{2,1,0:T(8,128)} %bitcast.4, f32[3,32,128]{2,1,0:T(8,128)} %medium_hbm.1, f32[16,32]{1,0:T(8,128)} %bitcast.5, f32[16,32]{1,0:T(8,128)} %bitcast.6, f32[4,128]{1,0:T(4,128)} %bitcast.7, bf16[2048,512]{1,0:T(8,128)(2,1)} %out_weight_hbm.1), custom_call_target="tpu_custom_call" | custom-call | tf_op jit(solution)/shard_map/pallas_call | solution.py:406
  64.2 0.7 %copy.9 = f32[256,256]{1,0:T(8,128)} copy(f32[256,256]{1,0:T(8,128)S(1)} %shard_map.73) | data formatting | bytes 524288

commit v5 on v4

--- a/solution.py
+++ b/solution.py
@@ -14,6 +14,7 @@
 LANES = 128
 ROW = 4
 RING = 4
+PARTS = 8
 SUB = 8
 
 
@@ -125,6 +126,10 @@
 
 def wrapped(index, count):
     return lax.rem(index + count, count)
+
+
+def farthest_first(count):
+    return sorted(range(1, count), key=lambda k: -min(k, count - k))
 
 
 def layer_kernel(
@@ -173,21 +178,23 @@
     loads += [pltpu.make_async_copy(a, b, local_sems.at[3 + k]) for k, (a, b) in enumerate(zip(whole, kept))]
     for i in (1, 2, 0, 3, 4, 5, 6, 7, 8):
         loads[i].start()
+    depth = channels // PARTS
     halo_copies = [
         [
             remote(
-                features_hbm.at[i, pl.ds(b * LANES, LANES), pl.ds(length - LANES, LANES)],
-                halo_ref.at[i, pl.ds(b * LANES, LANES)], halo_sems.at[i * blocks + b], following,
+                features_hbm.at[i, pl.ds(b * depth, depth), pl.ds(length - LANES, LANES)],
+                halo_ref.at[i, pl.ds(b * depth, depth)], halo_sems.at[i * PARTS + b], following,
             )
-            for b in range(blocks)
+            for b in range(PARTS)
         ]
         for i in range(3)
     ]
-    extra_copy = remote(packed_ref, extra_ref, halo_sems.at[3 * blocks], following)
+    extra_copy = remote(packed_ref, extra_ref, halo_sems.at[3 * PARTS], following)
     lane = iota((32, LANES), 1) // 8
     pl.semaphore_wait(barrier, len(peers))
-    halo_copies[1][0].start()
-    halo_copies[2][0].start()
+    for b in range(2):
+        halo_copies[1][b].start()
+        halo_copies[2][b].start()
     for i in (1, 2, 0):
         loads[i].wait()
         packed = jnp.zeros((32, LANES), jnp.float32)
@@ -196,10 +203,10 @@
             packed = jnp.where(lane == p, moved, packed)
         packed_ref[i] = packed
     extra_copy.start()
-    for b in range(1, blocks):
+    for b in range(2, PARTS):
         halo_copies[1][b].start()
         halo_copies[2][b].start()
-    for b in range(blocks):
+    for b in range(PARTS):
         halo_copies[0][b].start()
 
     signal(near_sems.at[3], at_row(1))
@@ -261,11 +268,12 @@
     pl.semaphore_wait(near_sems.at[2], 2)
     extra_copy.wait_recv()
     same = lax.rem(iota((LANES, LANES), 0), SUB) == iota((LANES, LANES), 1) // GROUP
-    quarter_steps = groups // blocks // 4
+    part_steps = groups // PARTS // 4
     for b in range(blocks):
-        halo_copies[1][b].wait_recv()
-        halo_copies[2][b].wait_recv()
-        lax.fori_loop(b * quarter_steps, (b + 1) * quarter_steps, product_step, 0)
+        for p in range(b * PARTS // blocks, (b + 1) * PARTS // blocks):
+            halo_copies[1][p].wait_recv()
+            halo_copies[2][p].wait_recv()
+            lax.fori_loop(p * part_steps, (p + 1) * part_steps, product_step, 0)
         rows = slice(b * LANES, (b + 1) * LANES)
         full = dot_split(split(ending_ref[rows, :]), split(product_ref[rows, :]), NT)
         full = jnp.where(same, full, 0.0)
@@ -273,8 +281,8 @@
     row_copies = [
         remote(state_ref, row_states_ref.at[k - 1], row_sems.at[k - 1], at_row(k)) for k in range(1, ROW)
     ]
-    for copy in row_copies:
-        copy.start()
+    for k in farthest_first(ROW):
+        row_copies[k - 1].start()
     for b in range(blocks):
         rows = slice(b * LANES, (b + 1) * LANES)
         gain = jnp.transpose(jnp.broadcast_to(gain_ref[b : b + 1, :], (LANES, LANES)))
@@ -297,8 +305,8 @@
         remote(total_ref.at[y], totals_ref.at[k - 1], column_sems.at[k - 1], at_column(k))
         for k in range(1, column)
     ]
-    for copy in column_copies:
-        copy.start()
+    for k in farthest_first(column):
+        column_copies[k - 1].start()
 
     for copy in halo_copies[0]:
         copy.wait_recv()
@@ -317,8 +325,8 @@
     start_copies = [
         remote(start_ref.at[y], start_ref.at[y], start_sems.at[k - 1], at_row(k)) for k in range(1, ROW)
     ]
-    for copy in start_copies:
-        copy.start()
+    for k in farthest_first(ROW):
+        start_copies[k - 1].start()
     for copy in start_copies:
         copy.wait_recv()
 
@@ -444,7 +452,7 @@
             pltpu.VMEM((2, part, length), f32),
             pltpu.SemaphoreType.REGULAR((4,)),
             pltpu.SemaphoreType.DMA((9,)),
-            pairs(3 * blocks + 1), pairs(ROW - 1), pairs(column - 1), pairs(ROW - 1), pairs(RING), pairs(6),
+            pairs(3 * PARTS + 1), pairs(ROW - 1), pairs(column - 1), pairs(ROW - 1), pairs(RING), pairs(6),
         ],
         compiler_params=pltpu.CompilerParams(
             collective_id=0, has_side_effects=True, vmem_limit_bytes=58 * 1024 * 1024

time: 65.1 us -> 62.9 us (0.966)
  Pallas kernels: 64.2 us -> 62.1 us
    pallas_call x1, Pallas kernels: 64.2 us -> 62.1 us  [per_device(): pl.pallas_call(layer_kernel, out_shape=pltpu.VMEM((part, length), f32), i...]
where the time goes in v5:
time: 62.9 us; the launch traced here: 62.8 us
  Pallas kernels  62.1 us (99%)
  local copies, waits for them, and re-layouts  0.71 us (1%)
    pallas_call x1, Pallas kernels, per_device(): pl.pallas_call(layer_kernel, out_shape=pltpu.VMEM((part, length), f32), i...  62.1 us

profile of v5, /device:TPU:1, one launch (start us, length us, event | category | flops | bytes accessed | tf_op | source)
XLA Modules:
  0.0 62.8 jit_solution(16599529671114346141)
XLA Ops:
  0.0 62.1 %shard_map.73 = f32[256,256]{1,0:T(8,128)S(1)} custom-call(f32[3,512,256]{2,1,0:T(8,128)} %features_hbm.1, f32[3,7,32]{2,1,0:T(8,128)} %bitcast.4, f32[3,32,128]{2,1,0:T(8,128)} %medium_hbm.1, f32[16,32]{1,0:T(8,128)} %bitcast.5, f32[16,32]{1,0:T(8,128)} %bitcast.6, f32[4,128]{1,0:T(4,128)} %bitcast.7, bf16[2048,512]{1,0:T(8,128)(2,1)} %out_weight_hbm.1), custom_call_target="tpu_custom_call" | custom-call | tf_op jit(solution)/shard_map/pallas_call | solution.py:414
  62.1 0.7 %copy.9 = f32[256,256]{1,0:T(8,128)} copy(f32[256,256]{1,0:T(8,128)S(1)} %shard_map.73) | data formatting | bytes 524288

commit v6 on v5

--- a/solution.py
+++ b/solution.py
@@ -189,7 +189,8 @@
         ]
         for i in range(3)
     ]
-    extra_copy = remote(packed_ref, extra_ref, halo_sems.at[3 * PARTS], following)
+    extra_copy = remote(packed_ref.at[pl.ds(1, 2)], extra_ref.at[pl.ds(1, 2)], halo_sems.at[3 * PARTS], following)
+    extra_last = remote(packed_ref.at[0], extra_ref.at[0], halo_sems.at[3 * PARTS + 1], following)
     lane = iota((32, LANES), 1) // 8
     pl.semaphore_wait(barrier, len(peers))
     for b in range(2):
@@ -202,10 +203,12 @@
             moved = pltpu.roll(features_ref[i, 32 * p : 32 * p + 32, 0:LANES], (8 * p + 8) % LANES, 1)
             packed = jnp.where(lane == p, moved, packed)
         packed_ref[i] = packed
-    extra_copy.start()
+        if i == 2:
+            extra_copy.start()
     for b in range(2, PARTS):
         halo_copies[1][b].start()
         halo_copies[2][b].start()
+    extra_last.start()
     for b in range(PARTS):
         halo_copies[0][b].start()
 
@@ -255,7 +258,12 @@
             value = branch(2, g, (matrix_high_ref[groups + g], matrix_low_ref[groups + g]))
             product = key * value
             product_ref[rows, :] = product
-            base_ref[rows, :] = long_group(product, (long_high_ref[g], long_low_ref[g]))
+        return carry
+
+    def base_step(half, carry):
+        for g in [half * 4 + u for u in range(4)]:
+            rows = pl.ds(pl.multiple_of(g * GROUP, GROUP), GROUP)
+            base_ref[rows, :] = long_group(product_ref[rows, :], (long_high_ref[g], long_low_ref[g]))
         return carry
 
     def query_step(half, carry):
@@ -283,10 +291,7 @@
     ]
     for k in farthest_first(ROW):
         row_copies[k - 1].start()
-    for b in range(blocks):
-        rows = slice(b * LANES, (b + 1) * LANES)
-        gain = jnp.transpose(jnp.broadcast_to(gain_ref[b : b + 1, :], (LANES, LANES)))
-        base_ref[rows, :] = base_ref[rows, :] + jnp.concatenate([gain] * (length // LANES), axis=1) * product_ref[rows, :]
+    lax.fori_loop(0, groups // 8, base_step, 0)
 
     rates = rate_blocks_ref[...]
     decay = lambda rates, steps: jnp.exp(-rates * (float(length) * steps))
@@ -310,7 +315,13 @@
 
     for copy in halo_copies[0]:
         copy.wait_recv()
+    extra_last.wait_recv()
     lax.fori_loop(0, groups // 2, query_step, 0)
+    lax.fori_loop(groups // 8, groups // 4, base_step, 0)
+    for b in range(blocks):
+        rows = slice(b * LANES, (b + 1) * LANES)
+        gain = jnp.transpose(jnp.broadcast_to(gain_ref[b : b + 1, :], (LANES, LANES)))
+        base_ref[rows, :] = base_ref[rows, :] + jnp.concatenate([gain] * (length // LANES), axis=1) * product_ref[rows, :]
 
     quarter = rate_blocks_ref[y]
     to_here = [
@@ -393,7 +404,7 @@
     late_down.wait_recv()
     out_ref[...] = mine_ref[0] + last_ref[0] + last_ref[1]
 
-    sent = halo_copies[0] + halo_copies[1] + halo_copies[2] + [extra_copy] + row_copies + column_copies + start_copies + pair_copies
+    sent = halo_copies[0] + halo_copies[1] + halo_copies[2] + [extra_copy, extra_last] + row_copies + column_copies + start_copies + pair_copies
     sent += [relay_up, relay_down, early_up, early_down, late_up, late_down]
     for copy in sent:
         copy.wait_send()
@@ -452,7 +463,7 @@
             pltpu.VMEM((2, part, length), f32),
             pltpu.SemaphoreType.REGULAR((4,)),
             pltpu.SemaphoreType.DMA((9,)),
-            pairs(3 * PARTS + 1), pairs(ROW - 1), pairs(column - 1), pairs(ROW - 1), pairs(RING), pairs(6),
+            pairs(3 * PARTS + 2), pairs(ROW - 1), pairs(column - 1), pairs(ROW - 1), pairs(RING), pairs(6),
         ],
         compiler_params=pltpu.CompilerParams(
             collective_id=0, has_side_effects=True, vmem_limit_bytes=58 * 1024 * 1024

time: 62.9 us -> 62.6 us (level)
  no operation moved by 1% of the time
where the time goes in v6:
time: 62.6 us; the launch traced here: 62.5 us
  Pallas kernels  61.8 us (99%)
  local copies, waits for them, and re-layouts  0.71 us (1%)
    pallas_call x1, Pallas kernels, per_device(): pl.pallas_call(layer_kernel, out_shape=pltpu.VMEM((part, length), f32), i...  61.8 us

profile of v6, /device:TPU:1, one launch (start us, length us, event | category | flops | bytes accessed | tf_op | source)
XLA Modules:
  0.0 62.5 jit_solution(10153775488053181492)
XLA Ops:
  0.0 61.8 %shard_map.73 = f32[256,256]{1,0:T(8,128)S(1)} custom-call(f32[3,512,256]{2,1,0:T(8,128)} %features_hbm.1, f32[3,7,32]{2,1,0:T(8,128)} %bitcast.4, f32[3,32,128]{2,1,0:T(8,128)} %medium_hbm.1, f32[16,32]{1,0:T(8,128)} %bitcast.5, f32[16,32]{1,0:T(8,128)} %bitcast.6, f32[4,128]{1,0:T(4,128)} %bitcast.7, bf16[2048,512]{1,0:T(8,128)(2,1)} %out_weight_hbm.1), custom_call_target="tpu_custom_call" | custom-call | tf_op jit(solution)/shard_map/pallas_call | solution.py:425
  61.8 0.7 %copy.9 = f32[256,256]{1,0:T(8,128)} copy(f32[256,256]{1,0:T(8,128)S(1)} %shard_map.73) | data formatting | bytes 524288
